TPU v7x, 256 devices: a whole 4x4x8 slice. The times are simulated.
256 devices in a mesh: chan: 8 (over z), ctx: 32 (over x, y, core).
Axes of the slice: x: 4, y: 4, z: 8, core: 2. Of those that a mesh axis runs over, the one named last changes fastest.
Arguments:
- projected: bfloat16 [32, 1024, 3, 4096], P('ctx', 'chan'), may hold values from -6 to 6
- short_taps: bfloat16 [3, 3, 4096], replicated, may hold values from -3 to 3
- long_filter: float32 [32768, 16], P('ctx', 'chan'), may hold values from -0.03125 to 0.03125
- skip_gain: float32 [4096], P('chan'), may hold values from -4 to 4
Outputs:
- gated: bfloat16 [32768, 4096], P('ctx', 'chan')
All inputs are finite; a program needn't handle non-finite values.
Results may differ from a plain program's by a relative error of at most 0.0064.
Values may be sent and summed in bfloat16 or wider, within the bound.
No kernel may reach another device: no remote copies, remote signals or barrier semaphores. Data moves between devices by JAX's collectives and lax.ppermute only.
A program may use at most 128 MiB of HBM per device.

v0:
```python
import math

import jax
import jax.numpy as jnp
from jax import lax
from jax.sharding import PartitionSpec as P

TAPS = 3


PRECISE = lax.Precision.HIGHEST


def passed_along(value, axis, by):
    count = lax.axis_size(axis)
    pairs = [(i, i + by) for i in range(count) if 0 <= i + by < count]
    return lax.ppermute(value, axis, pairs)


def counting(length):
    return jnp.arange(length, dtype=jnp.int32)


def phases(first, second, length):
    turned = first[:, None] * second[None, :] % length
    angles = turned.astype(jnp.float32) * (2.0 * math.pi / length)
    return (jnp.cos(angles), jnp.sin(angles))


def rotate(real_part, imag_part, cosines, sines, direction):
    return (
        real_part * cosines - direction * imag_part * sines,
        imag_part * cosines + direction * real_part * sines,
    )


def complex_mix(pattern, cosines, sines, real_part, imag_part, direction):
    cos_real = jnp.einsum(pattern, cosines, real_part, precision=PRECISE)
    sin_real = jnp.einsum(pattern, sines, real_part, precision=PRECISE)
    if imag_part is None:
        return (cos_real, direction * sin_real)
    cos_imag = jnp.einsum(pattern, cosines, imag_part, precision=PRECISE)
    sin_imag = jnp.einsum(pattern, sines, imag_part, precision=PRECISE)
    return (cos_real - direction * sin_imag, cos_imag + direction * sin_real)


def leading_factor(length):
    chosen = 1
    for option in range(1, math.isqrt(length) + 1):
        if length % option == 0:
            chosen = option
    return chosen


def local_tables(first, second):
    cos_one, sin_one = phases(counting(first), counting(first), first)
    cos_two, sin_two = phases(counting(second), counting(second), second)
    cos_mid, sin_mid = phases(counting(first), counting(second), first * second)
    return (
        cos_one,
        sin_one,
        cos_two,
        sin_two,
        cos_mid[None, :, :, None],
        sin_mid[None, :, :, None],
    )


def inner_forward(real_part, imag_part):
    leading, length, columns = real_part.shape
    first = leading_factor(length)
    second = length // first
    cos_one, sin_one, cos_two, sin_two, cos_mid, sin_mid = local_tables(first, second)
    real_part = real_part.reshape(leading, first, second, columns)
    real_part, imag_part = complex_mix(
        "bk,akjx->abjx", cos_one, sin_one, real_part, imag_part, -1.0
    )
    real_part, imag_part = rotate(real_part, imag_part, cos_mid, sin_mid, -1.0)
    return complex_mix("ej,abjx->abex", cos_two, sin_two, real_part, imag_part, -1.0)


def inner_inverse(real_part, imag_part):
    leading, first, second, columns = real_part.shape
    cos_one, sin_one, cos_two, sin_two, cos_mid, sin_mid = local_tables(first, second)
    real_part, imag_part = complex_mix("ej,abjx->abex", cos_two, sin_two, real_part, imag_part, 1.0)
    real_part, imag_part = rotate(real_part, imag_part, cos_mid, sin_mid, 1.0)
    real_part, imag_part = complex_mix("kb,abjx->akjx", cos_one, sin_one, real_part, imag_part, 1.0)
    return (
        real_part.reshape(leading, first * second, columns),
        imag_part.reshape(leading, first * second, columns),
    )


def featurize(earlier, own_rows, filter_taps):
    lag_rows = earlier.shape[0]
    length = own_rows.shape[0]
    extended = jnp.concatenate([earlier, own_rows], axis=0).astype(jnp.float32)
    weights = filter_taps.astype(jnp.float32)
    summed = weights[0] * extended[lag_rows : lag_rows + length]
    for offset in range(1, weights.shape[0]):
        summed = summed + weights[offset] * extended[lag_rows - offset : lag_rows - offset + length]
    queries = lax.optimization_barrier(summed[:, 0].astype(jnp.bfloat16))
    product = (summed[:, 1] * summed[:, 2]).astype(jnp.bfloat16)
    return (queries, product)


def whole_transform(real_part):
    zeros = jnp.zeros_like(real_part)
    padded_real = jnp.concatenate([real_part, zeros], axis=0)[None]
    padded_imag = None
    return inner_forward(padded_real, padded_imag)


def local_convolve(signal, filters, gains_here, position, per_group):
    length, columns = signal.shape
    groups_here = filters.shape[1]
    first_channel = position * columns
    owners = (first_channel + counting(columns)) // per_group
    selector = (counting(groups_here)[:, None] == owners[None, :]).astype(jnp.float32)
    filt_real, filt_imag = whole_transform(filters)
    filt_real = jnp.einsum("abex,xc->abec", filt_real, selector, precision=PRECISE)
    filt_imag = jnp.einsum("abex,xc->abec", filt_imag, selector, precision=PRECISE)
    sig_real, sig_imag = whole_transform(signal)
    prod_real = sig_real * filt_real - sig_imag * filt_imag
    prod_imag = sig_real * filt_imag + sig_imag * filt_real
    back_real, back_imag = inner_inverse(prod_real, prod_imag)
    inverse_scale = 1.0 / (2 * length)
    conv_real = back_real[0, :length] * inverse_scale
    return conv_real + gains_here * signal


def local(projected, short_taps, long_filter, skip_gain):
    devices = lax.axis_size("ctx")
    position = lax.axis_index("ctx")
    channel_slot = lax.axis_index("chan")
    channels = skip_gain.shape[0]
    groups_here = long_filter.shape[1]
    per_group = channels // groups_here
    regrouped = lax.all_to_all(projected, "chan", split_axis=3, concat_axis=1, tiled=True)[0]
    taps_here = lax.dynamic_slice_in_dim(short_taps, channel_slot * channels, channels, 2)
    last_rows = regrouped[regrouped.shape[0] - (TAPS - 1) :]
    earlier = passed_along(last_rows, "ctx", 1)
    queries, product = featurize(earlier, regrouped, taps_here)
    kv_seq = lax.all_to_all(product[None], "ctx", split_axis=2, concat_axis=0, tiled=True)
    block_rows = kv_seq.shape[1]
    columns = kv_seq.shape[2]
    signal = kv_seq.reshape(devices * block_rows, columns).astype(jnp.float32)
    filters = lax.all_gather(long_filter, "ctx", axis=0, tiled=True)
    gains_here = lax.dynamic_slice_in_dim(skip_gain, position * columns, columns, 0)
    mixed = local_convolve(signal, filters, gains_here, position, per_group).astype(jnp.bfloat16)
    mixed = mixed.reshape(devices, block_rows, columns)
    mixed_rows = lax.all_to_all(mixed, "ctx", split_axis=0, concat_axis=2, tiled=True)[0]
    return (queries.astype(jnp.float32) * mixed_rows.astype(jnp.float32)).astype(jnp.bfloat16)


def solution(mesh):
    placed = (P("ctx", "chan", None, None), P(), P("ctx", "chan"), P("chan"))
    return jax.shard_map(
        local, mesh=mesh, in_specs=placed, out_specs=P("ctx", "chan"), check_vma=False
    )
```

profile of v0, /device:TPU:1, one launch (start us, length us, event | category | flops | bytes accessed | tf_op | source)
XLA Modules:
  0.0 315.8 jit_solution(2454380333297750385)
XLA Ops:
  0.0 7.2 %copy.59 = bf16[1,128,3,4096]{1,2,0,3:T(4,128)(2,1)} copy(bf16[1,128,3,4096]{3,1,2,0:T(8,128)(2,1)} %param.4) | data formatting | bytes 6291456 | tf_op args[0]
  7.2 9.1 %all-to-all-start = ((bf16[1,128,3,4096]{1,2,0,3:T(4,128)(2,1)}), bf16[1,128,3,4096]{1,2,0,3:T(4,128)(2,1)}, u32[]{:S(2)}, u32[]{:S(2)}) async-start(bf16[1,128,3,4096]{1,2,0,3:T(4,128)(2,1)} %copy.59), calls=%async_computation | async-start | bytes 8388608 | tf_op jit(solution)/shard_map/all_to_all | solution.py:139
  20.5 26.1 %all_gather.3 = f32[32768,2]{0,1:T(2,128)S(1)} all-gather(f32[1024,2]{0,1:T(2,128)S(1)} %copy-done.20), channel_id=1, replica_groups=mesh['chan'=8,'ctx'=32] {'ctx'}, dimensions={0}, use_global_device_ids=true | all-gather | bytes 270336 | tf_op jit(solution)/shard_map/all_gather | solution.py:148
  58.5 54.7 %all-to-all-done = bf16[1,128,3,4096]{1,2,0,3:T(4,128)(2,1)} async-done(((bf16[1,128,3,4096]{1,2,0,3:T(4,128)(2,1)}), bf16[1,128,3,4096]{1,2,0,3:T(4,128)(2,1)}, u32[]{:S(2)}, u32[]{:S(2)}) %all-to-all-start) | async-done | bytes 3145760 | tf_op jit(solution)/shard_map/all_to_all | solution.py:139
  113.2 6.8 %copy.131 = bf16[1,128,3,8,512]{1,3,4,2,0:T(8,128)(2,1)} copy(bf16[1,128,3,8,512]{1,2,4,3,0:T(4,128)(2,1)} %bitcast.1) | data formatting | bytes 6291456 | tf_op jit(solution)/shard_map/all_to_all | solution.py:139
  120.0 4.1 %squeeze.2 = bf16[1024,3,512]{0,2,1:T(8,128)(2,1)S(1)} reshape(bf16[1,8,128,3,512]{2,1,4,3,0:T(8,128)(2,1)} %bitcast.281) | data formatting | bytes 6291456 | tf_op jit(solution)/shard_map/squeeze | solution.py:139
  128.7 5.0 %collective-permute-done = bf16[2,3,512]{0,2,1:T(8,128)(2,1)} collective-permute-done((bf16[2,3,512]{0,2,1:T(8,128)(2,1)}, bf16[2,3,512]{0,2,1:T(8,128)(2,1)}, u32[]{:S(2)}, u32[]{:S(2)}) %collective-permute-start) | collective-permute-done | bytes 6176 | tf_op jit(solution)/shard_map/ppermute | solution.py:17
  136.4 5.1 %fusion = f32[1024,3,512]{0,2,1:T(8,128)S(1)} fusion(f32[1026,3,512]{0,2,1:T(8,128)S(1)} %maximum_convert_fusion, f32[3,512]{1,0:T(4,128)S(1)} %get-tuple-element.8, f32[3,512]{1,0:T(4,128)S(1)} %get-tuple-element.9, f32[3,512]{1,0:T(4,128)S(1)} %get-tuple-element.7), kind=kLoop, calls=%fused_computation.1 | loop fusion | flops 7864320 | bytes 25184256 | tf_op jit(solution)/shard_map/add | solution.py:101
  144.6 7.7 %reduce = bf16[512,1024]{1,0:T(8,128)(2,1)} reduce(bf16[512,1,1024]{2,1,0:T(2,128)(2,1)S(1)} %bitcast.285, bf16[]{:T(256)} %broadcast.317), dimensions={1}, to_apply=%bitcast.278.reduce_sub_computation | reduce | bytes 2097154
  155.0 8.8 %all-to-all-start.1 = ((bf16[32,2,8192]{2,1,0:T(2,128)(2,1)}), bf16[32,2,8192]{2,1,0:T(2,128)(2,1)}, u32[]{:S(2)}, u32[]{:S(2)}) async-start(bf16[32,2,8192]{2,1,0:T(2,128)(2,1)} %reshape.221), calls=%async_computation.1 | async-start | bytes 2097152 | tf_op jit(solution)/shard_map/all_to_all | solution.py:144
  174.5 6.1 %all-to-all-done.1 = bf16[32,2,8192]{2,1,0:T(2,128)(2,1)} async-done(((bf16[32,2,8192]{2,1,0:T(2,128)(2,1)}), bf16[32,2,8192]{2,1,0:T(2,128)(2,1)}, u32[]{:S(2)}, u32[]{:S(2)}) %all-to-all-start.1) | async-done | bytes 1048608 | tf_op jit(solution)/shard_map/all_to_all | solution.py:144
  180.6 4.3 %reshape.222 = bf16[512,1,1024]{2,1,0:T(2,128)(2,1)S(1)} reshape(bf16[32,2,8192]{2,1,0:T(2,128)(2,1)} %all-to-all-done.1) | data formatting | bytes 2097152
  192.9 8.4 %fusion.48 = f32[256,16,256]{2,0,1:T(8,128)S(1)} fusion(f32[256,16,256]{2,0,1:T(8,128)S(1)} %fusion.94, f32[256,16,256]{2,0,1:T(8,128)S(1)} %fusion.83, f32[256,256]{0,1:T(8,128)S(1)} %copy-done.11, f32[256,256]{0,1:T(8,128)S(1)} %copy-done.13), kind=kOutput, calls=%fused_computation.65 | convolution fusion | flops 3225288704 | bytes 13107200 | tf_op jit(solution)/shard_map/ej,abjx->abex/dot_general | solution.py:39
  201.3 10.6 %fusion.50 = f32[256,16,256]{2,0,1:T(8,128)} fusion(f32[256,16,256]{2,0,1:T(8,128)S(1)} %fusion.94, f32[256,16,256]{2,0,1:T(8,128)S(1)} %fusion.83, f32[256,256]{0,1:T(8,128)S(1)} %copy-done.11, f32[256,256]{0,1:T(8,128)S(1)} %copy-done.13), kind=kOutput, calls=%fused_computation.66 | convolution fusion | flops 3225288704 | bytes 13107200 | tf_op jit(solution)/shard_map/ej,abjx->abex/dot_general | solution.py:38
  211.9 9.9 %multiply_add_fusion = f32[256,16,256]{2,0,1:T(8,128)} fusion(f32[256,16,256]{2,0,1:T(8,128)S(1)} %fusion.48, f32[256,16,256]{2,0,1:T(8,128)S(1)} %fusion.94, f32[256,16,256]{2,0,1:T(8,128)S(1)} %fusion.83, f32[256,256]{0,1:T(8,128)S(1)} %copy-done.9, f32[256,256]{0,1:T(8,128)S(1)} %copy-done.6), kind=kOutput, calls=%fused_computation.38 | convolution fusion | flops 3227385856 | bytes 17301504 | tf_op jit(solution)/shard_map/ej,abjx->abex/dot_general | solution.py:42
  221.7 18.6 %fusion.16 = (f32[1,256,256,16]{2,1,3,0:T(8,128)S(1)}, f32[256,256,16]{1,0,2:T(8,128)S(1)}) fusion(f32[256,16,256]{2,0,1:T(8,128)} %multiply_add_fusion, f32[256,256,16]{1,2,0:T(8,128)} %fusion.64, f32[256,256,16]{1,2,0:T(8,128)} %fusion.66, f32[256,16,256]{2,0,1:T(8,128)} %fusion.50, f32[256,256]{0,1:T(8,128)} %copy-done.7, ...), kind=kOutput, calls=%fused_computation.23 | convolution fusion | flops 3233677312 | bytes 34078720 | tf_op jit(solution)/shard_map/ej,abjx->abex/dot_general | solution.py:43
  240.4 4.7 %fusion.75 = f32[256,16,256]{2,0,1:T(8,128)S(1)} fusion(f32[256,256,16]{1,0,2:T(8,128)S(1)} %get-tuple-element.6), kind=kOutput, calls=%fused_computation.96 | convolution fusion | flops 3222142976 | bytes 8388608 | tf_op jit(solution)/shard_map/ej,abjx->abex/dot_general | solution.py:39
  245.1 4.4 %fusion.87 = f32[256,16,256]{2,0,1:T(8,128)S(1)} fusion(f32[256,256,16]{1,0,2:T(8,128)S(1)} %get-tuple-element.6), kind=kOutput, calls=%fused_computation.108 | convolution fusion | flops 3222142976 | bytes 8388608 | tf_op jit(solution)/shard_map/ej,abjx->abex/dot_general | solution.py:38
  249.5 5.2 %fusion.31 = f32[256,16,256]{2,0,1:T(8,128)S(1)} fusion(f32[256,16,256]{2,0,1:T(8,128)S(1)} %fusion.75, f32[1,256,256,16]{2,1,3,0:T(8,128)S(1)} %get-tuple-element.5), kind=kOutput, calls=%fused_computation.43 | convolution fusion | flops 3223191552 | bytes 12582912 | tf_op jit(solution)/shard_map/ej,abjx->abex/dot_general | solution.py:42
  254.7 4.8 %fusion.28 = f32[256,16,256]{2,0,1:T(8,128)S(1)} fusion(f32[256,16,256]{2,0,1:T(8,128)S(1)} %fusion.87, f32[1,256,256,16]{2,1,3,0:T(8,128)S(1)} %get-tuple-element.5), kind=kOutput, calls=%fused_computation.42 | convolution fusion | flops 3223191552 | bytes 12582912 | tf_op jit(solution)/shard_map/ej,abjx->abex/dot_general | solution.py:43
  259.6 8.3 %fusion.2 = f32[256,16,256]{2,0,1:T(8,128)S(1)} fusion(f32[256,16,256]{2,0,1:T(8,128)S(1)} %fusion.31, f32[256,16,256]{2,0,1:T(8,128)S(1)} %fusion.28, f32[256,256]{1,0:T(8,128)S(1)} %copy-done.15, f32[256,256]{1,0:T(8,128)S(1)} %copy-done.17), kind=kOutput, calls=%fused_computation.5 | convolution fusion | flops 3225288704 | bytes 13107200 | tf_op jit(solution)/shard_map/kb,abjx->akjx/dot_general | solution.py:43
  267.9 10.3 %subtract_bitcast_fusion = f32[1,256,256,16]{1,2,3,0:T(8,128)} fusion(f32[256,16,256]{2,0,1:T(8,128)S(1)} %fusion.2, f32[256,16,256]{2,0,1:T(8,128)S(1)} %fusion.31, f32[256,16,256]{2,0,1:T(8,128)S(1)} %fusion.28, f32[256,256]{1,0:T(8,128)S(1)} %copy-done.15, f32[256,256]{1,0:T(8,128)S(1)} %copy-done.17), kind=kOutput, calls=%fused_computation.37 | convolution fusion | flops 3226337280 | bytes 17301504 | tf_op jit(solution)/shard_map/kb,abjx->akjx/dot_general | solution.py:38
  278.1 5.4 %copy.89 = f32[1,256,256,16]{2,1,3,0:T(8,128)} copy(f32[1,256,256,16]{1,2,3,0:T(8,128)} %subtract_bitcast_fusion) | data formatting | bytes 8388608 | tf_op jit(solution)/shard_map/sub | solution.py:44
  298.4 15.2 %all-to-all-done.2 = bf16[32,1024,16]{1,2,0:T(8,128)(2,1)S(1)} async-done(((bf16[32,1024,16]{1,2,0:T(8,128)(2,1)}), bf16[32,1024,16]{1,2,0:T(8,128)(2,1)S(1)}, u32[]{:S(2)}, u32[]{:S(2)}) %all-to-all-start.2) | async-done | bytes 1048608 | tf_op jit(solution)/shard_map/all_to_all | solution.py:152
  (84 shorter events, 64.3 us)
Async XLA Ops:
  7.2 13.3 %copy-start.20 = (f32[1024,2]{0,1:T(2,128)S(1)}, f32[1024,2]{0,1:T(2,128)}, u32[]{:S(2)}) copy-start(f32[1024,2]{0,1:T(2,128)} %param.6) | copy-start | bytes 24580
  7.2 106.0 %all-to-all-start = ((bf16[1,128,3,4096]{1,2,0,3:T(4,128)(2,1)}), bf16[1,128,3,4096]{1,2,0,3:T(4,128)(2,1)}, u32[]{:S(2)}, u32[]{:S(2)}) async-start(bf16[1,128,3,4096]{1,2,0,3:T(4,128)(2,1)} %copy.59), calls=%async_computation | async-start | bytes 8388608 | tf_op jit(solution)/shard_map/all_to_all | solution.py:139
  17.5 147.2 %copy-start.5 = (f32[256,256]{0,1:T(8,128)}, f32[256,256]{0,1:T(8,128)S(1)}, u32[]{:S(2)}) copy-start(f32[256,256]{0,1:T(8,128)S(1)} %copy.68) | copy-start | bytes 786436
  18.6 37.2 %copy-start.7 = (f32[256,256]{0,1:T(8,128)}, f32[256,256]{0,1:T(8,128)S(1)}, u32[]{:S(2)}) copy-start(f32[256,256]{0,1:T(8,128)S(1)} %copy.69) | copy-start | bytes 786436
  19.7 36.1 %copy-start.16 = (f32[256,256]{1,0:T(8,128)}, f32[256,256]{1,0:T(8,128)S(1)}, u32[]{:S(2)}) copy-start(f32[256,256]{1,0:T(8,128)S(1)} %get-tuple-element.11) | copy-start | bytes 786436
  20.4 35.5 %copy-start.10 = (f32[256,256]{0,1:T(8,128)}, f32[256,256]{0,1:T(8,128)S(1)}, u32[]{:S(2)}) copy-start(f32[256,256]{0,1:T(8,128)S(1)} %copy.66) | copy-start | bytes 786436
  20.5 38.0 %copy-start.12 = (f32[256,256]{0,1:T(8,128)}, f32[256,256]{0,1:T(8,128)S(1)}, u32[]{:S(2)}) copy-start(f32[256,256]{0,1:T(8,128)S(1)} %copy.64) | copy-start | bytes 786436
  49.4 6.5 %copy-start.1 = (f32[1,256,256,2]{1,2,3,0:T(8,128)}, f32[1,256,256,2]{1,2,3,0:T(8,128)S(1)}, u32[]{:S(2)}) copy-start(f32[1,256,256,2]{1,2,3,0:T(8,128)S(1)} %convolution_bitcast_fusion) | copy-start | bytes 1572868
  51.2 4.6 %copy-start.3 = (f32[1,256,256,2]{1,2,3,0:T(8,128)}, f32[1,256,256,2]{1,2,3,0:T(8,128)S(1)}, u32[]{:S(2)}) copy-start(f32[1,256,256,2]{1,2,3,0:T(8,128)S(1)} %convolution_bitcast_fusion.1) | copy-start | bytes 1572868
  125.1 8.6 %collective-permute-start = (bf16[2,3,512]{0,2,1:T(8,128)(2,1)}, bf16[2,3,512]{0,2,1:T(8,128)(2,1)}, u32[]{:S(2)}, u32[]{:S(2)}) collective-permute-start(bf16[2,3,512]{0,2,1:T(8,128)(2,1)} %slice.46), channel_id=1, source_target_pairs={{0,1},{1,2},{2,3},{3,4},{4,5},{5,6},{6,7},{7,8},{8,9},{9,10},{10,1... | collective-permute-start | bytes 18440 | tf_op jit(solution)/shard_map/ppermute | solution.py:17
  141.4 2.6 copy-start
  144.1 20.6 %copy-start.2 = (f32[1,256,256,2]{1,2,3,0:T(8,128)S(1)}, f32[1,256,256,2]{1,2,3,0:T(8,128)}, u32[]{:S(2)}) copy-start(f32[1,256,256,2]{1,2,3,0:T(8,128)} %copy-done.1) | copy-start | bytes 1572868
  144.1 20.6 %copy-start.4 = (f32[1,256,256,2]{1,2,3,0:T(8,128)S(1)}, f32[1,256,256,2]{1,2,3,0:T(8,128)}, u32[]{:S(2)}) copy-start(f32[1,256,256,2]{1,2,3,0:T(8,128)} %copy-done.3) | copy-start | bytes 1572868
  152.3 12.3 %copy-start.8 = (f32[256,256]{0,1:T(8,128)S(1)}, f32[256,256]{0,1:T(8,128)}, u32[]{:S(2)}) copy-start(f32[256,256]{0,1:T(8,128)} %copy-done.7) | copy-start | bytes 786436
  152.3 12.4 %copy-start.19 = (f32[256,2,256]{2,0,1:T(8,128)S(1)}, f32[256,2,256]{2,0,1:T(8,128)}, u32[]{:S(2)}) copy-start(f32[256,2,256]{2,0,1:T(8,128)} %fusion.62) | copy-start | bytes 1572868
  155.0 25.6 %all-to-all-start.1 = ((bf16[32,2,8192]{2,1,0:T(2,128)(2,1)}), bf16[32,2,8192]{2,1,0:T(2,128)(2,1)}, u32[]{:S(2)}, u32[]{:S(2)}) async-start(bf16[32,2,8192]{2,1,0:T(2,128)(2,1)} %reshape.221), calls=%async_computation.1 | async-start | bytes 2097152 | tf_op jit(solution)/shard_map/all_to_all | solution.py:144
  163.8 6.7 %copy-start.18 = (f32[256,256,2]{1,0,2:T(8,128)S(1)}, f32[256,256,2]{1,0,2:T(8,128)}, u32[]{:S(2)}) copy-start(f32[256,256,2]{1,0,2:T(8,128)} %fusion.45) | copy-start | bytes 1572868
  189.4 3.4 %copy-start.11 = (f32[256,256]{0,1:T(8,128)S(1)}, f32[256,256]{0,1:T(8,128)}, u32[]{:S(2)}) copy-start(f32[256,256]{0,1:T(8,128)} %copy-done.10) | copy-start | bytes 786436
  189.4 3.4 %copy-start.13 = (f32[256,256]{0,1:T(8,128)S(1)}, f32[256,256]{0,1:T(8,128)}, u32[]{:S(2)}) copy-start(f32[256,256]{0,1:T(8,128)} %copy-done.12) | copy-start | bytes 786436
  201.3 10.6 %copy-start.6 = (f32[256,256]{0,1:T(8,128)S(1)}, f32[256,256]{0,1:T(8,128)}, u32[]{:S(2)}) copy-start(f32[256,256]{0,1:T(8,128)} %copy-done.5) | copy-start | bytes 786436
  201.3 10.6 %copy-start.9 = (f32[256,256]{0,1:T(8,128)S(1)}, f32[256,256]{0,1:T(8,128)}, u32[]{:S(2)}) copy-start(f32[256,256]{0,1:T(8,128)} %copy-done.7) | copy-start | bytes 786436
  254.7 4.9 %copy-start.15 = (f32[256,256]{1,0:T(8,128)S(1)}, f32[256,256]{1,0:T(8,128)}, u32[]{:S(2)}) copy-start(f32[256,256]{1,0:T(8,128)} %copy-done.14) | copy-start | bytes 786436
  254.7 4.9 %copy-start.17 = (f32[256,256]{1,0:T(8,128)S(1)}, f32[256,256]{1,0:T(8,128)}, u32[]{:S(2)}) copy-start(f32[256,256]{1,0:T(8,128)} %copy-done.16) | copy-start | bytes 786436
  292.8 20.8 %all-to-all-start.2 = ((bf16[32,1024,16]{1,2,0:T(8,128)(2,1)}), bf16[32,1024,16]{1,2,0:T(8,128)(2,1)S(1)}, u32[]{:S(2)}, u32[]{:S(2)}) async-start(bf16[32,1024,16]{1,2,0:T(8,128)(2,1)} %fusion.37), calls=%async_computation.2 | async-start | bytes 2097152 | tf_op jit(solution)/shard_map/all_to_all | solution.py:152
  (1 other events, 0.7 us)
where the time goes:
time: 320 us; the launch traced here: 316 us
  matrix products  113 us (35%)
  waiting for transfers between devices  81 us (25%)
  local copies, waits for them, and re-layouts  45.8 us (14%)
  blocking collectives  26.1 us (8%)
  starting transfers between devices  25.4 us (8%)
  other arithmetic  24.1 us (8%)
    all_to_all x1, waiting for transfers between devices, local(): lax.all_to_all(projected, 'chan', split_axis=3, concat_axis=1, tiled=True)  54.7 us
    dot_general x4, matrix products, complex_mix(): sin_imag = jnp.einsum(pattern, sines, imag_part, precision=PRECISE)  33.7 us
    dot_general x6, matrix products, complex_mix(): cos_real = jnp.einsum(pattern, cosines, real_part, precision=PRECISE)  33.2 us
    all_gather x1, blocking collectives, local(): filters = lax.all_gather(long_filter, 'ctx', axis=0, tiled=True)  26.1 us
    dot_general x5, matrix products, complex_mix(): sin_real = jnp.einsum(pattern, sines, real_part, precision=PRECISE)  20.9 us
    unnamed x50, local copies, waits for them, and re-layouts  18.2 us
    dot_general x3, matrix products, complex_mix(): cos_imag = jnp.einsum(pattern, cosines, imag_part, precision=PRECISE)  16.9 us
    all_to_all x1, waiting for transfers between devices, local(): lax.all_to_all(mixed, 'ctx', split_axis=0, concat_axis=2, tiled=True)[0]  15.2 us
  transfers between devices with their start and end apart: 4, of which 4 were waited for; matrix products, arithmetic and copies ran while one was open for 9% of the time, Pallas kernels for 0%

commit v1 on v0

v1 whole, which is shorter than its diff:
```python
import jax
import jax.numpy as jnp
from jax import lax
from jax.experimental import pallas as pl
from jax.experimental.pallas import tpu as pltpu
from jax.sharding import PartitionSpec as P


F32 = jnp.float32
BF16 = jnp.bfloat16
TILE = 128
GROUP_DEPTH = 8
ROW_CHUNK = 512
BIG = pltpu.CompilerParams(vmem_limit_bytes=60 * 1024 * 1024)
WHOLE = pl.BlockSpec(memory_space=pltpu.VMEM)


def estimate(flops, moved):
    return pl.CostEstimate(flops=flops, bytes_accessed=moved, transcendentals=0)


def featurize_kernel(x_ref, before_ref, taps_ref, query_ref, kv_ref):
    taps, _, columns = taps_ref.shape
    rows = x_ref.shape[1]
    index = lax.broadcasted_iota(jnp.int32, (rows, columns), 0)

    def feature(which):
        own = x_ref[which].astype(F32)
        before = before_ref[which].astype(F32)
        weights = taps_ref[:, which].astype(F32)
        total = weights[0:1] * own
        for lag in range(1, taps):
            moved = pltpu.roll(own, lag, 0)
            for row in range(lag):
                source = taps - 1 - lag + row
                moved = jnp.where(index == row, before[source : source + 1], moved)
            total = total + weights[lag : lag + 1] * moved
        return total

    query_ref[0] = feature(0).astype(BF16)
    product = feature(1) * feature(2)
    kv_ref[...] = product.T.astype(BF16).reshape(kv_ref.shape)


def featurize(own, before, taps, slots, per_device):
    streams, rows, channels = own.shape
    lags = taps.shape[0]
    columns = channels // slots
    pieces = columns // per_device
    return pl.pallas_call(
        featurize_kernel,
        grid=(slots,),
        out_shape=(
            jax.ShapeDtypeStruct((slots, rows, columns), BF16),
            jax.ShapeDtypeStruct((slots * pieces, per_device, rows), BF16),
        ),
        in_specs=[
            pl.BlockSpec((streams, rows, columns), lambda i: (0, 0, i)),
            pl.BlockSpec((streams, lags - 1, columns), lambda i: (0, 0, i)),
            pl.BlockSpec((lags, streams, columns), lambda i: (0, 0, i)),
        ],
        out_specs=(
            pl.BlockSpec((1, rows, columns), lambda i: (i, 0, 0)),
            pl.BlockSpec((pieces, per_device, rows), lambda i: (i, 0, 0)),
        ),
        cost_estimate=estimate(20 * own.size, 4 * own.size),
        name="featurize",
    )(own, before, taps)


def toeplitz_kernel(lags_ref, out_ref):
    count, tile = lags_ref.shape
    unroll = 8
    upper = lax.broadcasted_iota(jnp.int32, (tile, tile), 1) >= lax.broadcasted_iota(
        jnp.int32, (tile, tile), 0
    )
    zeros = jnp.zeros((tile, tile), F32)
    out_ref[0:tile, :] = zeros.astype(BF16)

    def step(index, earlier):
        first = pl.multiple_of(index * unroll, unroll)
        lines = lags_ref[pl.ds(first, unroll), :].astype(F32)
        for part in range(unroll):
            spread = jnp.broadcast_to(lines[part : part + 1], (tile, tile))
            turned = pltpu.roll(spread, 0, 1, stride=1, stride_axis=0)
            place = pl.multiple_of((first + part + 1) * tile, tile)
            out_ref[pl.ds(place, tile), :] = jnp.where(upper, turned, earlier).astype(BF16)
            earlier = turned
        return earlier

    lax.fori_loop(0, count // unroll, step, zeros)


def toeplitz(lags):
    count, tile = lags.shape
    size = (count + 1) * tile
    return pl.pallas_call(
        toeplitz_kernel,
        out_shape=jax.ShapeDtypeStruct((size, tile), BF16),
        in_specs=[WHOLE],
        out_specs=WHOLE,
        compiler_params=BIG,
        cost_estimate=estimate(4 * size * tile, 2 * size * tile),
        name="toeplitz",
    )(lags)


def convolve_kernel(x_ref, weights_ref, gain_ref, out_ref, wide_ref, total_ref):
    slots, devices, channels, tile = x_ref.shape
    pairs = slots * devices // 2
    depth = wide_ref.shape[1]
    taken = depth // tile
    group = taken // 2
    for part in range(taken):
        lanes = slice(part * tile, (part + 1) * tile)
        for pair in range(pairs):
            rows = slice(pair * channels, (pair + 1) * channels)
            block = 2 * pair + 1 - part
            if block < 0:
                wide_ref[rows, lanes] = jnp.zeros((channels, tile), BF16)
            else:
                wide_ref[rows, lanes] = x_ref[block % slots, block // slots]
    total_ref[...] = jnp.zeros_like(total_ref)
    height = pairs * channels
    stride = group * channels

    def step(index, carry):
        base = pl.multiple_of(index * depth, depth)
        next_base = pl.multiple_of(base + tile, tile)
        weights = jnp.concatenate(
            [weights_ref[pl.ds(base, depth), :], weights_ref[pl.ds(next_base, depth), :]], axis=1
        )
        chunks = (height - index * stride + ROW_CHUNK - 1) // ROW_CHUNK

        def rows_step(chunk, inner):
            source = pl.multiple_of(chunk * ROW_CHUNK, ROW_CHUNK)
            target = pl.ds(pl.multiple_of(source + index * stride, stride), ROW_CHUNK)
            total_ref[target, :] += jnp.dot(
                wide_ref[pl.ds(source, ROW_CHUNK), :], weights, preferred_element_type=F32
            )
            return inner

        return lax.fori_loop(0, chunks, rows_step, carry)

    lax.fori_loop(0, pairs // group, step, 0)
    gain = gain_ref[...]
    for block in range(2 * pairs):
        half = slice((block % 2) * tile, (block % 2 + 1) * tile)
        rows = slice((block // 2) * channels, (block // 2 + 1) * channels)
        direct = gain * x_ref[block % slots, block // slots].astype(F32)
        out_ref[block] = (total_ref[rows, half] + direct).astype(BF16)


def convolve(x, weights, gain):
    slots, devices, channels, tile = x.shape
    blocks = slots * devices
    height = blocks // 2 * channels
    depth = 2 * GROUP_DEPTH * tile
    return pl.pallas_call(
        convolve_kernel,
        out_shape=jax.ShapeDtypeStruct((blocks, channels, tile), BF16),
        in_specs=[WHOLE] * 3,
        out_specs=WHOLE,
        scratch_shapes=[
            pltpu.VMEM((height, depth), BF16),
            pltpu.VMEM((height + ROW_CHUNK, 2 * tile), F32),
        ],
        compiler_params=BIG,
        cost_estimate=estimate(blocks * blocks * channels * tile * tile, 4 * x.size + 2 * weights.size),
        name="convolve",
    )(x, weights, gain)


def gate_kernel(query_ref, mixed_ref, out_ref):
    columns = out_ref.shape[1]
    mixed = mixed_ref[:, 0].reshape(columns, -1).astype(F32)
    out_ref[...] = (query_ref[0].astype(F32) * mixed.T).astype(BF16)


def gate(query, mixed):
    slots, rows, columns = query.shape
    devices, _, channels, _ = mixed.shape
    return pl.pallas_call(
        gate_kernel,
        grid=(slots,),
        out_shape=jax.ShapeDtypeStruct((slots * rows, columns), BF16),
        in_specs=[
            pl.BlockSpec((1, rows, columns), lambda i: (i, 0, 0)),
            pl.BlockSpec((devices, 1, channels, rows), lambda i: (0, i, 0, 0)),
        ],
        out_specs=pl.BlockSpec((rows, columns), lambda i: (i, 0)),
        cost_estimate=estimate(2 * query.size, 6 * query.size),
        name="gate",
    )(query, mixed)


def stages(projected, short_taps, long_filter, skip_gain):
    devices = lax.axis_size("ctx")
    slots = lax.axis_size("chan")
    own = jnp.transpose(projected[0], (1, 0, 2))
    rows = own.shape[1]
    columns = skip_gain.shape[0]
    channels = columns // devices
    lags = short_taps.shape[0]

    order = [(t % slots) * devices + t // slots for t in range(slots * devices)]
    before = lax.ppermute(own[:, rows - (lags - 1) :], ("chan", "ctx"), list(zip(order, order[1:])))

    here = long_filter.shape[1]
    lines = jnp.repeat(long_filter.T.astype(BF16), devices // here, axis=0)
    lines = lines.reshape(devices, -1, TILE)
    lines = lax.all_to_all(lines, "ctx", 0, 0, tiled=True).reshape(-1, TILE)

    query, kv = featurize(own, before, short_taps, slots, channels)
    lines, kv = lax.optimization_barrier((lines, kv))
    weights = toeplitz(lines)
    kv = lax.all_to_all(kv, ("chan", "ctx"), 0, 0, tiled=True)
    query, kv = lax.optimization_barrier((query, kv))
    query = lax.all_to_all(query, "chan", 0, 0, tiled=True)

    gains = lax.dynamic_slice_in_dim(skip_gain, lax.axis_index("ctx") * channels, channels)
    gains = jnp.broadcast_to(gains[:, None], (channels, TILE))
    mixed = convolve(kv.reshape(slots, devices, channels, rows), weights, gains)
    mixed, query = lax.optimization_barrier((mixed, query))
    mixed = mixed.reshape(devices, slots, channels, rows)
    mixed = lax.all_to_all(mixed, "ctx", 0, 0, tiled=True)
    return gate(query, mixed)


def solution(mesh):
    placed = (P("ctx", "chan", None, None), P(), P("ctx", "chan"), P("chan"))
    return jax.shard_map(
        stages, mesh=mesh, in_specs=placed, out_specs=P("ctx", "chan"), check_vma=False
    )
```

time: 320 us -> 152 us (0.47)
  matrix products: 113 us -> 0 us
  waiting for transfers between devices: 81 us -> 5.94 us
  Pallas kernels: 0 us -> 59.2 us
  local copies, waits for them, and re-layouts: 45.8 us -> 3.67 us
  blocking collectives: 26.1 us -> 65 us
  other arithmetic: 24.1 us -> 0.7 us
  starting transfers between devices: 25.4 us -> 16.2 us
    dot_general x20 -> x0, matrix products: 113 us -> none  [the longest x4 33.7 us: complex_mix(): sin_imag = jnp.einsum(pattern, sines, imag_part, precision=PRECISE)]
    all_to_all x3 -> x2, waiting for transfers between devices: 76 us -> 0.01 us  [the longest x1 0.01 us: stages(): lines = lax.all_to_all(lines, 'ctx', 0, 0, tiled=True).reshape(-1, TILE)]
    all_to_all x0 -> x2, blocking collectives: none -> 65 us  [the longest x1 42.7 us: stages(): kv = lax.all_to_all(kv, ('chan', 'ctx'), 0, 0, tiled=True)]
    pallas_call x0 -> x4, Pallas kernels: none -> 59.2 us  [the longest x1 36.9 us: convolve(): pl.pallas_call(convolve_kernel, out_shape=jax.ShapeDtypeStruct((blocks, c...]
    all_gather x1 -> x0, blocking collectives: 26.1 us -> none  [local(): filters = lax.all_gather(long_filter, 'ctx', axis=0, tiled=True)]
    unnamed x50 -> x7, local copies, waits for them, and re-layouts: 18.2 us -> 1.26 us
    all_to_all x3 -> x2, starting transfers between devices: 21.8 us -> 12.7 us  [the longest x1 8.58 us: stages(): lines = lax.all_to_all(lines, 'ctx', 0, 0, tiled=True).reshape(-1, TILE)]
    unnamed x1 -> x0, other arithmetic: 7.72 us -> none
  transfers between devices with their start and end apart: 4 -> 3, of which waited for: 4 -> 1; matrix products, arithmetic and copies ran while one was open for 9% -> 2% of each run, Pallas kernels for 0% -> 35%
where the time goes in v1:
time: 152 us; the launch traced here: 151 us
  blocking collectives  65 us (43%)
  Pallas kernels  59.2 us (39%)
  starting transfers between devices  16.2 us (11%)
  waiting for transfers between devices  5.94 us (4%)
  local copies, waits for them, and re-layouts  3.67 us (2%)
    all_to_all x1, blocking collectives, stages(): kv = lax.all_to_all(kv, ('chan', 'ctx'), 0, 0, tiled=True)  42.7 us
    pallas_call x1, Pallas kernels, convolve(): pl.pallas_call(convolve_kernel, out_shape=jax.ShapeDtypeStruct((blocks, c...  36.9 us
    all_to_all x1, blocking collectives, stages(): mixed = lax.all_to_all(mixed, 'ctx', 0, 0, tiled=True)  22.3 us
    pallas_call x1, Pallas kernels, toeplitz(): pl.pallas_call(toeplitz_kernel, out_shape=jax.ShapeDtypeStruct((size, til...  9.05 us
    all_to_all x1, starting transfers between devices, stages(): lines = lax.all_to_all(lines, 'ctx', 0, 0, tiled=True).reshape(-1, TILE)  8.58 us
    pallas_call x1, Pallas kernels, featurize(): pl.pallas_call(featurize_kernel, grid=(slots,), out_shape=(jax.ShapeDtype...  7.37 us
    ppermute x1, waiting for transfers between devices, stages(): lax.ppermute(own[:, rows - (lags - 1):], ('chan', 'ctx'), list(zip(order,...  5.93 us
    pallas_call x1, Pallas kernels, gate(): pl.pallas_call(gate_kernel, grid=(slots,), out_shape=jax.ShapeDtypeStruct...  5.85 us
  transfers between devices with their start and end apart: 3, of which 1 were waited for; matrix products, arithmetic and copies ran while one was open for 2% of the time, Pallas kernels for 35%

profile of v1, /device:TPU:1, one launch (start us, length us, event | category | flops | bytes accessed | tf_op | source)
XLA Modules:
  0.0 150.7 jit_solution(14030585169606695864)
XLA Ops:
  0.0 0.7 convert_bitcast_fusion
  0.7 0.6 copy.5
  1.3 8.6 %all-to-all-start = ((bf16[32,8,128]{2,1,0:T(8,128)(2,1)}), bf16[32,8,128]{2,1,0:T(8,128)(2,1)S(1)}, u32[]{:S(2)}, u32[]{:S(2)}) async-start(bf16[32,8,128]{2,1,0:T(8,128)(2,1)} %bitcast.9), calls=%async_computation | async-start | bytes 131072 | tf_op jit(solution)/shard_map/all_to_all | solution.py:212
  9.9 1.0 slice.4
  10.9 3.5 %collective-permute-start = (bf16[3,2,4096]{2,1,0:T(2,128)(2,1)S(1)}, bf16[3,2,4096]{2,1,0:T(2,128)(2,1)S(1)}, u32[]{:S(2)}, u32[]{:S(2)}) collective-permute-start(bf16[3,2,4096]{2,1,0:T(2,128)(2,1)S(1)} %slice.4), channel_id=1, source_target_pairs={{0,32},{32,64},{64,96},{96,128},{128,160},{160,192},{192,224},{224... | collective-permute-start | bytes 147464 | tf_op jit(solution)/shard_map/ppermute | solution.py:207
  14.5 5.9 %collective-permute-done.before_ref = bf16[3,2,4096]{2,1,0:T(2,128)(2,1)S(1)} collective-permute-done((bf16[3,2,4096]{2,1,0:T(2,128)(2,1)S(1)}, bf16[3,2,4096]{2,1,0:T(2,128)(2,1)S(1)}, u32[]{:S(2)}, u32[]{:S(2)}) %collective-permute-start) | collective-permute-done | bytes 49184 | tf_op jit(solution)/shard_map/ppermute | solution.py:207
  20.4 0.0 copy-start.2
  20.4 0.6 copy-done.2
  21.0 7.4 %featurize.1 = (bf16[8,128,512]{2,1,0:T(8,128)(2,1)}, bf16[256,16,128]{2,1,0:T(8,128)(2,1)}) custom-call(bf16[3,128,4096]{2,1,0:T(8,128)(2,1)} %bitcast.12, bf16[3,2,4096]{2,1,0:T(2,128)(2,1)} %copy-done.2, bf16[3,3,4096]{2,1,0:T(4,128)(2,1)} %taps_ref.1), custom_call_target="tpu_custom_call" | custom-call | flops 31457280 | bytes 6291456 | tf_op jit(solution)/shard_map/featurize/pallas_call | solution.py:50
  28.4 0.0 all-to-all-done
  28.4 0.0 copy-start.1
  28.4 42.7 %all_to_all.20 = bf16[256,16,128]{2,1,0:T(8,128)(2,1)} all-to-all(bf16[256,16,128]{2,1,0:T(8,128)(2,1)} %get-tuple-element.15), channel_id=1, replica_groups=mesh['chan'=8,'ctx'=32] {'chan','ctx'}, dimensions={0} | all-to-all | bytes 2097152 | tf_op jit(solution)/shard_map/all_to_all | solution.py:217
  71.1 4.1 %all-to-all-start.2 = ((bf16[8,128,512]{2,1,0:T(8,128)(2,1)}), bf16[8,128,512]{2,1,0:T(8,128)(2,1)S(1)}, u32[]{:S(2)}, u32[]{:S(2)}) async-start(bf16[8,128,512]{2,1,0:T(8,128)(2,1)} %get-tuple-element.18), calls=%async_computation.2 | async-start | bytes 2097152 | tf_op jit(solution)/shard_map/all_to_all | solution.py:219
  75.2 0.8 dynamic_slice.3
  75.9 0.0 copy-done.1
  75.9 9.0 %toeplitz.1.weights_ref = bf16[32896,128]{1,0:T(8,128)(2,1)} custom-call(bf16[256,128]{1,0:T(8,128)(2,1)} %bitcast.15), custom_call_target="tpu_custom_call" | custom-call | flops 16842752 | bytes 8421376 | tf_op jit(solution)/shard_map/toeplitz/pallas_call | solution.py:97
  85.0 0.7 broadcast_in_dim.10.gain_ref
  85.6 36.9 %convolve.1 = bf16[256,16,128]{2,1,0:T(8,128)(2,1)} custom-call(bf16[8,32,16,128]{3,2,1,0:T(8,128)(2,1)} %bitcast.13, bf16[32896,128]{1,0:T(8,128)(2,1)} %toeplitz.1.weights_ref, f32[16,128]{1,0:T(8,128)} %broadcast_in_dim.10.gain_ref), custom_call_target="tpu_custom_call" | custom-call | flops 17179869184 | bytes 10518528 | tf_op jit(solution)/shard_map/convolve/pallas_call | solution.py:159
  122.6 0.0 all-to-all-done.2.query_ref
  122.6 0.0 copy-start
  122.6 22.3 %all_to_all.21.mixed_ref = bf16[32,8,16,128]{3,2,1,0:T(8,128)(2,1)} all-to-all(bf16[32,8,16,128]{3,2,1,0:T(8,128)(2,1)} %bitcast.14), channel_id=1, replica_groups=mesh['chan'=8,'ctx'=32] {'ctx'}, dimensions={0} | all-to-all | bytes 2097152 | tf_op jit(solution)/shard_map/all_to_all | solution.py:226
  144.9 0.0 copy-done
  144.9 5.9 %gate.1 = bf16[1024,512]{1,0:T(8,128)(2,1)} custom-call(bf16[8,128,512]{2,1,0:T(8,128)(2,1)} %copy-done, bf16[32,8,16,128]{3,2,1,0:T(8,128)(2,1)} %all_to_all.21.mixed_ref), custom_call_target="tpu_custom_call" | custom-call | flops 1048576 | bytes 3145728 | tf_op jit(solution)/shard_map/gate/pallas_call | solution.py:183
  (1 shorter events, 0.0 us)
Async XLA Ops:
  1.3 27.0 %all-to-all-start = ((bf16[32,8,128]{2,1,0:T(8,128)(2,1)}), bf16[32,8,128]{2,1,0:T(8,128)(2,1)S(1)}, u32[]{:S(2)}, u32[]{:S(2)}) async-start(bf16[32,8,128]{2,1,0:T(8,128)(2,1)} %bitcast.9), calls=%async_computation | async-start | bytes 131072 | tf_op jit(solution)/shard_map/all_to_all | solution.py:212
  10.9 9.5 %collective-permute-start = (bf16[3,2,4096]{2,1,0:T(2,128)(2,1)S(1)}, bf16[3,2,4096]{2,1,0:T(2,128)(2,1)S(1)}, u32[]{:S(2)}, u32[]{:S(2)}) collective-permute-start(bf16[3,2,4096]{2,1,0:T(2,128)(2,1)S(1)} %slice.4), channel_id=1, source_target_pairs={{0,32},{32,64},{64,96},{96,128},{128,160},{160,192},{192,224},{224... | collective-permute-start | bytes 147464 | tf_op jit(solution)/shard_map/ppermute | solution.py:207
  20.4 0.6 copy-start.2
  28.4 47.5 %copy-start.1 = (bf16[32,8,128]{2,1,0:T(8,128)(2,1)}, bf16[32,8,128]{2,1,0:T(8,128)(2,1)S(1)}, u32[]{:S(2)}) copy-start(bf16[32,8,128]{2,1,0:T(8,128)(2,1)S(1)} %all-to-all-done) | copy-start | bytes 196612
  71.1 51.5 %all-to-all-start.2 = ((bf16[8,128,512]{2,1,0:T(8,128)(2,1)}), bf16[8,128,512]{2,1,0:T(8,128)(2,1)S(1)}, u32[]{:S(2)}, u32[]{:S(2)}) async-start(bf16[8,128,512]{2,1,0:T(8,128)(2,1)} %get-tuple-element.18), calls=%async_computation.2 | async-start | bytes 2097152 | tf_op jit(solution)/shard_map/all_to_all | solution.py:219
  122.6 22.3 %copy-start = (bf16[8,128,512]{2,1,0:T(8,128)(2,1)}, bf16[8,128,512]{2,1,0:T(8,128)(2,1)S(1)}, u32[]{:S(2)}) copy-start(bf16[8,128,512]{2,1,0:T(8,128)(2,1)S(1)} %all-to-all-done.2.query_ref) | copy-start | bytes 3145732

commit v2 on v1

v2 whole, which is shorter than its diff:
```python
import functools

import jax
import jax.numpy as jnp
from jax import lax
from jax.experimental import pallas as pl
from jax.experimental.pallas import tpu as pltpu
from jax.sharding import PartitionSpec as P


F32 = jnp.float32
BF16 = jnp.bfloat16
TILE = 128
GROUP_DEPTH = 32
ROW_CHUNK = 512
BIG = pltpu.CompilerParams(vmem_limit_bytes=60 * 1024 * 1024)
WHOLE = pl.BlockSpec(memory_space=pltpu.VMEM)


def estimate(flops, moved):
    return pl.CostEstimate(flops=flops, bytes_accessed=moved, transcendentals=0)


def transposed(value):
    size = value.shape[1]
    ones = lax.broadcasted_iota(jnp.int32, (size, size), 0) == lax.broadcasted_iota(
        jnp.int32, (size, size), 1
    )
    return lax.dot_general(
        ones.astype(BF16), value, (((1,), (1,)), ((), ())), preferred_element_type=F32
    )


def featurize_kernel(here_ref, x_ref, before_ref, taps_ref, query_ref, kv_ref):
    taps, _, columns = taps_ref.shape
    rows = x_ref.shape[1]
    tile = 8
    index = lax.broadcasted_iota(jnp.int32, (tile, columns), 0)

    def feature(which):
        own = x_ref[which].astype(F32)
        before = before_ref[which].astype(F32)
        weights = taps_ref[:, which].astype(F32)
        total = weights[0:1] * own
        for lag in range(1, taps):
            moved = pltpu.roll(own, lag, 0)
            top = moved[:tile]
            for row in range(lag):
                source = taps - 1 - lag + row
                top = jnp.where(index == row, before[source : source + 1], top)
            moved = jnp.concatenate([top, moved[tile:]], axis=0)
            total = total + weights[lag : lag + 1] * moved
        return total

    query_ref[0] = feature(0).astype(BF16)
    product = (feature(1) * feature(2)).astype(BF16)
    _, per_device, _ = kv_ref.shape
    count = TILE // per_device
    for part in range(columns // TILE):
        turned = transposed(product[:, part * TILE : (part + 1) * TILE]).astype(BF16)
        kv_ref[part * count : (part + 1) * count] = turned.reshape(count, per_device, rows)


def featurize(here, own, before, taps, slots, per_device):
    streams, rows, channels = own.shape
    lags = taps.shape[0]
    columns = channels // slots
    pieces = columns // per_device
    return pl.pallas_call(
        featurize_kernel,
        grid_spec=pltpu.PrefetchScalarGridSpec(
            num_scalar_prefetch=1,
            grid=(slots,),
            in_specs=[
                pl.BlockSpec((streams, rows, columns), lambda i, here: (0, 0, i)),
                pl.BlockSpec((streams, lags - 1, columns), lambda i, here: (0, 0, i)),
                pl.BlockSpec((lags, streams, columns), lambda i, here: (0, 0, i)),
            ],
            out_specs=(
                pl.BlockSpec(
                    (1, rows, columns), lambda i, here: ((i + slots - here[0]) % slots, 0, 0)
                ),
                pl.BlockSpec((pieces, per_device, rows), lambda i, here: (i, 0, 0)),
            ),
        ),
        out_shape=(
            jax.ShapeDtypeStruct((slots, rows, columns), BF16),
            jax.ShapeDtypeStruct((slots * pieces, per_device, rows), BF16),
        ),
        cost_estimate=estimate(20 * own.size, 4 * own.size),
        name="featurize",
    )(here, own, before, taps)


def toeplitz_kernel(lags_ref, out_ref):
    count, tile = lags_ref.shape
    unroll = 8
    upper = lax.broadcasted_iota(jnp.int32, (tile, tile), 1) >= lax.broadcasted_iota(
        jnp.int32, (tile, tile), 0
    )
    zeros = jnp.zeros((tile, tile), F32)
    out_ref[0:tile, :] = zeros.astype(BF16)

    def step(index, earlier):
        first = pl.multiple_of(index * unroll, unroll)
        lines = lags_ref[pl.ds(first, unroll), :].astype(F32)
        for part in range(unroll):
            spread = jnp.broadcast_to(lines[part : part + 1], (tile, tile))
            turned = pltpu.roll(spread, 0, 1, stride=1, stride_axis=0)
            place = pl.multiple_of((first + part + 1) * tile, tile)
            out_ref[pl.ds(place, tile), :] = jnp.where(upper, turned, earlier).astype(BF16)
            earlier = turned
        return earlier

    lax.fori_loop(0, count // unroll, step, zeros)


def toeplitz(lags):
    count, tile = lags.shape
    size = (count + 1) * tile
    return pl.pallas_call(
        toeplitz_kernel,
        out_shape=jax.ShapeDtypeStruct((size, tile), BF16),
        in_specs=[WHOLE],
        out_specs=WHOLE,
        compiler_params=BIG,
        cost_estimate=estimate(4 * size * tile, 2 * size * tile),
        name="toeplitz",
    )(lags)


def convolve_kernel(x_ref, weights_ref, gain_ref, out_ref, pair_ref, total_ref, *, margin, group):
    slots, devices, channels, tile = x_ref.shape
    pairs = slots * devices // 2
    pair_ref[0:margin, :] = jnp.zeros((margin, 2 * tile), BF16)
    for pair in range(pairs):
        start = margin + pair * channels
        for half in range(2):
            block = 2 * pair + 1 - half
            lanes = slice(half * tile, (half + 1) * tile)
            pair_ref[start : start + channels, lanes] = x_ref[block % slots, block // slots]
    depth = 2 * group * tile
    stride = group * channels
    gain = gain_ref[...]
    for top in range(0, pairs * channels, ROW_CHUNK):

        def step(index, carry, top=top):
            base = pl.multiple_of(index * depth, depth)
            next_base = pl.multiple_of(base + tile, tile)
            weights = jnp.concatenate(
                [weights_ref[pl.ds(base, depth), :], weights_ref[pl.ds(next_base, depth), :]],
                axis=1,
            )
            parts = []
            for part in range(group):
                start = pl.multiple_of(margin + top - index * stride - part * channels, channels)
                parts.append(pair_ref[pl.ds(start, ROW_CHUNK), :])
            total_ref[...] += jnp.dot(
                jnp.concatenate(parts, axis=1), weights, preferred_element_type=F32
            )
            return carry

        total_ref[...] = jnp.zeros_like(total_ref)
        lax.fori_loop(0, (top + ROW_CHUNK + stride - 1) // stride, step, 0)
        for pair in range(ROW_CHUNK // channels):
            rows = slice(pair * channels, (pair + 1) * channels)
            for half in range(2):
                block = 2 * (top // channels + pair) + half
                lanes = slice(half * tile, (half + 1) * tile)
                direct = gain * x_ref[block % slots, block // slots].astype(F32)
                out_ref[block] = (total_ref[rows, lanes] + direct).astype(BF16)


def convolve(x, weights, gain):
    slots, devices, channels, tile = x.shape
    blocks = slots * devices
    height = blocks // 2 * channels
    margin = max(GROUP_DEPTH * channels, ROW_CHUNK)
    return pl.pallas_call(
        functools.partial(convolve_kernel, margin=margin, group=GROUP_DEPTH),
        out_shape=jax.ShapeDtypeStruct((blocks, channels, tile), BF16),
        in_specs=[WHOLE] * 3,
        out_specs=WHOLE,
        scratch_shapes=[
            pltpu.VMEM((height + margin, 2 * tile), BF16),
            pltpu.VMEM((ROW_CHUNK, 2 * tile), F32),
        ],
        compiler_params=BIG,
        cost_estimate=estimate(blocks * blocks * channels * tile * tile, 4 * x.size + 2 * weights.size),
        name="convolve",
    )(x, weights, gain)


def gate_kernel(here_ref, *refs):
    queries, mixed_ref, out_ref = refs[:-2], refs[-2], refs[-1]
    slots = len(queries)
    rows, columns = queries[0].shape
    for shift, query_ref in enumerate(queries):
        slot = (here_ref[0] + slots - shift) % slots
        mixed = mixed_ref[:, pl.ds(slot, 1)].reshape(columns, rows)
        target = pl.ds(pl.multiple_of(slot * rows, rows), rows)
        out_ref[target, :] = (query_ref[...].astype(F32) * transposed(mixed)).astype(BF16)


def gate(here, queries, mixed):
    rows, columns = queries[0].shape
    total = len(queries) * rows
    return pl.pallas_call(
        gate_kernel,
        out_shape=jax.ShapeDtypeStruct((total, columns), BF16),
        in_specs=[pl.BlockSpec(memory_space=pltpu.SMEM)] + [WHOLE] * (len(queries) + 1),
        out_specs=WHOLE,
        compiler_params=pltpu.CompilerParams(vmem_limit_bytes=16 * 1024 * 1024),
        cost_estimate=estimate(2 * total * columns, 6 * total * columns),
        name="gate",
    )(here, *queries, mixed)


def stages(projected, short_taps, long_filter, skip_gain):
    devices = lax.axis_size("ctx")
    slots = lax.axis_size("chan")
    own = jnp.transpose(projected[0], (1, 0, 2))
    rows = own.shape[1]
    columns = skip_gain.shape[0]
    channels = columns // devices
    lags = short_taps.shape[0]
    here = lax.axis_index("chan").astype(jnp.int32).reshape(1)

    order = [(t % slots) * devices + t // slots for t in range(slots * devices)]
    pairs = list(zip(order, order[1:]))
    before = lax.ppermute(own[:, rows - (lags - 1) :], ("chan", "ctx"), pairs)

    groups = long_filter.shape[1]
    lines = jnp.repeat(long_filter.T.astype(BF16), devices // groups, axis=0)
    lines = lines.reshape(devices, -1, TILE)
    lines = lax.all_to_all(lines, "ctx", 0, 0, tiled=True).reshape(-1, TILE)

    query, kv = featurize(here, own, before, short_taps, slots, channels)
    lines, kv = lax.optimization_barrier((lines, kv))
    weights = toeplitz(lines)
    kv = lax.all_to_all(kv, ("chan", "ctx"), 0, 0, tiled=True)
    queries = [query[0]]
    for shift in range(1, slots):
        ring = [(i, (i + shift) % slots) for i in range(slots)]
        queries.append(lax.ppermute(query[shift], "chan", ring))

    gains = lax.dynamic_slice_in_dim(skip_gain, lax.axis_index("ctx") * channels, channels)
    gains = jnp.broadcast_to(gains[:, None], (channels, TILE))
    mixed = convolve(kv.reshape(slots, devices, channels, rows), weights, gains)
    mixed = mixed.reshape(devices, slots, channels, rows)
    mixed = lax.all_to_all(mixed, "ctx", 0, 0, tiled=True)
    return gate(here, queries, mixed)


def solution(mesh):
    placed = (P("ctx", "chan", None, None), P(), P("ctx", "chan"), P("chan"))
    return jax.shard_map(
        stages, mesh=mesh, in_specs=placed, out_specs=P("ctx", "chan"), check_vma=False
    )
```

time: 152 us -> 140 us (0.921)
  blocking collectives: 65 us -> 0 us
  waiting for transfers between devices: 5.94 us -> 47.2 us
  starting transfers between devices: 16.2 us -> 40.3 us
  Pallas kernels: 59.2 us -> 46.8 us
    all_to_all x2 -> x0, blocking collectives: 65 us -> none  [the longest x1 42.7 us: stages(): kv = lax.all_to_all(kv, ('chan', 'ctx'), 0, 0, tiled=True)]
    ppermute x1 -> x8, waiting for transfers between devices: 5.93 us -> 26.6 us  [the longest x7 20.7 us: stages(): queries.append(lax.ppermute(query[shift], 'chan', ring))]
    all_to_all x1 -> x2, waiting for transfers between devices: 0.01 us -> 20.6 us  [the longest x1 20.6 us: stages(): kv = lax.all_to_all(kv, ('chan', 'ctx'), 0, 0, tiled=True)]
    all_to_all x1 -> x2, starting transfers between devices: 4.08 us -> 17.8 us  [the longest x1 12.2 us: stages(): kv = lax.all_to_all(kv, ('chan', 'ctx'), 0, 0, tiled=True)]
    pallas_call x3, Pallas kernels: 50.2 us -> 37.7 us  [the longest x1 28.7 us: convolve(): pl.pallas_call(functools.partial(convolve_kernel, margin=margin, group=GR...]
    ppermute x1 -> x8, starting transfers between devices: 3.55 us -> 13.9 us  [the longest x7 10.3 us: stages(): queries.append(lax.ppermute(query[shift], 'chan', ring))]
  transfers between devices with their start and end apart: 3 -> 11, of which waited for: 1 -> 6; matrix products, arithmetic and copies ran while one was open for 2% -> 1% of each run, Pallas kernels for 35% -> 12%
where the time goes in v2:
time: 140 us; the launch traced here: 139 us
  waiting for transfers between devices  47.2 us (34%)
  Pallas kernels  46.8 us (33%)
  starting transfers between devices  40.3 us (29%)
  local copies, waits for them, and re-layouts  4.19 us (3%)
    pallas_call x1, Pallas kernels, convolve(): pl.pallas_call(functools.partial(convolve_kernel, margin=margin, group=GR...  28.7 us
    ppermute x7, waiting for transfers between devices, stages(): queries.append(lax.ppermute(query[shift], 'chan', ring))  20.7 us
    all_to_all x1, waiting for transfers between devices, stages(): kv = lax.all_to_all(kv, ('chan', 'ctx'), 0, 0, tiled=True)  20.6 us
    all_to_all x1, starting transfers between devices, stages(): kv = lax.all_to_all(kv, ('chan', 'ctx'), 0, 0, tiled=True)  12.2 us
    ppermute x7, starting transfers between devices, stages(): queries.append(lax.ppermute(query[shift], 'chan', ring))  10.3 us
    pallas_call x1, Pallas kernels, toeplitz(): pl.pallas_call(toeplitz_kernel, out_shape=jax.ShapeDtypeStruct((size, til...  9.07 us
    all_to_all x1, starting transfers between devices, stages(): lines = lax.all_to_all(lines, 'ctx', 0, 0, tiled=True).reshape(-1, TILE)  8.58 us
    pallas_call x1, Pallas kernels, featurize(): pl.pallas_call(featurize_kernel, grid_spec=pltpu.PrefetchScalarGridSpec(n...  7.59 us
  transfers between devices with their start and end apart: 11, of which 6 were waited for; matrix products, arithmetic and copies ran while one was open for 1% of the time, Pallas kernels for 12%

profile of v2, /device:TPU:1, one launch (start us, length us, event | category | flops | bytes accessed | tf_op | source)
XLA Modules:
  0.0 139.2 jit_solution(1057559069821885987)
XLA Ops:
  0.0 0.7 convert_bitcast_fusion
  0.7 0.6 copy.5
  1.4 8.6 %all-to-all-start = ((bf16[32,8,128]{2,1,0:T(8,128)(2,1)}), bf16[32,8,128]{2,1,0:T(8,128)(2,1)S(1)}, u32[]{:S(2)}, u32[]{:S(2)}) async-start(bf16[32,8,128]{2,1,0:T(8,128)(2,1)} %bitcast.18), calls=%async_computation | async-start | bytes 131072 | tf_op jit(solution)/shard_map/all_to_all | solution.py:236
  9.9 1.0 slice.36
  10.9 3.5 %collective-permute-start = (bf16[3,2,4096]{2,1,0:T(2,128)(2,1)S(1)}, bf16[3,2,4096]{2,1,0:T(2,128)(2,1)S(1)}, u32[]{:S(2)}, u32[]{:S(2)}) collective-permute-start(bf16[3,2,4096]{2,1,0:T(2,128)(2,1)S(1)} %slice.36), channel_id=1, source_target_pairs={{0,32},{32,64},{64,96},{96,128},{128,160},{160,192},{192,224},{224... | collective-permute-start | bytes 147464 | tf_op jit(solution)/shard_map/ppermute | solution.py:231
  14.5 5.9 %collective-permute-done.before_ref = bf16[3,2,4096]{2,1,0:T(2,128)(2,1)S(1)} collective-permute-done((bf16[3,2,4096]{2,1,0:T(2,128)(2,1)S(1)}, bf16[3,2,4096]{2,1,0:T(2,128)(2,1)S(1)}, u32[]{:S(2)}, u32[]{:S(2)}) %collective-permute-start) | collective-permute-done | bytes 49184 | tf_op jit(solution)/shard_map/ppermute | solution.py:231
  21.0 7.6 %featurize.1 = (bf16[8,128,512]{2,1,0:T(8,128)(2,1)}, bf16[256,16,128]{2,1,0:T(8,128)(2,1)}) custom-call(s32[1]{0:T(128)} %bitcast.here_ref, bf16[3,128,4096]{2,1,0:T(8,128)(2,1)} %bitcast.29, bf16[3,2,4096]{2,1,0:T(2,128)(2,1)} %copy-done.3, bf16[3,3,4096]{2,1,0:T(4,128)(2,1)} %taps_ref.1), custom_call_target="tpu_custom_call" | custom-call | flops 31457280 | bytes 6291456 | tf_op jit(solution)/shard_map/featurize/pallas_call | solution.py:69
  28.6 12.2 %all-to-all-start.1 = ((bf16[256,16,128]{2,1,0:T(8,128)(2,1)}), bf16[256,16,128]{2,1,0:T(8,128)(2,1)S(1)}, u32[]{:S(2)}, u32[]{:S(2)}) async-start(bf16[256,16,128]{2,1,0:T(8,128)(2,1)} %get-tuple-element.11), calls=%async_computation.1 | async-start | bytes 2097152 | tf_op jit(solution)/shard_map/all_to_all | solution.py:241
  40.8 0.8 dynamic_slice.3
  41.6 9.1 %toeplitz.1.weights_ref = bf16[32896,128]{1,0:T(8,128)(2,1)} custom-call(bf16[256,128]{1,0:T(8,128)(2,1)} %bitcast.32), custom_call_target="tpu_custom_call" | custom-call | flops 16842752 | bytes 8421376 | tf_op jit(solution)/shard_map/toeplitz/pallas_call | solution.py:121
  50.6 20.6 %all-to-all-done.1 = bf16[256,16,128]{2,1,0:T(8,128)(2,1)S(1)} async-done(((bf16[256,16,128]{2,1,0:T(8,128)(2,1)}), bf16[256,16,128]{2,1,0:T(8,128)(2,1)S(1)}, u32[]{:S(2)}, u32[]{:S(2)}) %all-to-all-start.1) | async-done | bytes 1048608 | tf_op jit(solution)/shard_map/all_to_all | solution.py:241
  71.2 0.8 broadcast_in_dim.10.gain_ref
  72.3 28.7 %convolve.1 = bf16[256,16,128]{2,1,0:T(8,128)(2,1)} custom-call(bf16[8,32,16,128]{3,2,1,0:T(8,128)(2,1)} %bitcast.31, bf16[32896,128]{1,0:T(8,128)(2,1)} %toeplitz.1.weights_ref, f32[16,128]{1,0:T(8,128)} %broadcast_in_dim.10.gain_ref), custom_call_target="tpu_custom_call" | custom-call | flops 17179869184 | bytes 10518528 | tf_op jit(solution)/shard_map/convolve/pallas_call | solution.py:179
  101.0 5.6 %all-to-all-start.2 = ((bf16[32,8,16,128]{3,2,1,0:T(8,128)(2,1)}), bf16[32,8,16,128]{3,2,1,0:T(8,128)(2,1)S(1)}, u32[]{:S(2)}, u32[]{:S(2)}) async-start(bf16[32,8,16,128]{3,2,1,0:T(8,128)(2,1)} %bitcast.30), calls=%async_computation.2 | async-start | bytes 2097152 | tf_op jit(solution)/shard_map/all_to_all | solution.py:251
  106.7 1.2 collective-permute-start.7
  107.9 2.9 %collective-permute-start.5 = (bf16[128,512]{1,0:T(8,128)(2,1)S(1)}, bf16[128,512]{1,0:T(8,128)(2,1)S(1)}, u32[]{:S(2)}, u32[]{:S(2)}) collective-permute-start(bf16[128,512]{1,0:T(8,128)(2,1)S(1)} %get-tuple-element.15), channel_id=1, source_target_pairs={{0,160},{32,192},{64,224},{96,0},{128,32},{160,64},{192,96},{224,1... | collective-permute-start | bytes 393224 | tf_op jit(solution)/shard_map/ppermute | solution.py:245
  110.8 2.6 %collective-permute-start.4 = (bf16[128,512]{1,0:T(8,128)(2,1)S(1)}, bf16[128,512]{1,0:T(8,128)(2,1)S(1)}, u32[]{:S(2)}, u32[]{:S(2)}) collective-permute-start(bf16[128,512]{1,0:T(8,128)(2,1)S(1)} %get-tuple-element.16), channel_id=1, source_target_pairs={{0,128},{32,160},{64,192},{96,224},{128,0},{160,32},{192,64},{224,... | collective-permute-start | bytes 393224 | tf_op jit(solution)/shard_map/ppermute | solution.py:245
  113.4 2.0 %collective-permute-start.3 = (bf16[128,512]{1,0:T(8,128)(2,1)S(1)}, bf16[128,512]{1,0:T(8,128)(2,1)S(1)}, u32[]{:S(2)}, u32[]{:S(2)}) collective-permute-start(bf16[128,512]{1,0:T(8,128)(2,1)S(1)} %get-tuple-element.17), channel_id=1, source_target_pairs={{0,96},{32,128},{64,160},{96,192},{128,224},{160,0},{192,32},{224,... | collective-permute-start | bytes 393224 | tf_op jit(solution)/shard_map/ppermute | solution.py:245
  115.4 1.7 %collective-permute-start.2 = (bf16[128,512]{1,0:T(8,128)(2,1)S(1)}, bf16[128,512]{1,0:T(8,128)(2,1)S(1)}, u32[]{:S(2)}, u32[]{:S(2)}) collective-permute-start(bf16[128,512]{1,0:T(8,128)(2,1)S(1)} %get-tuple-element.18), channel_id=1, source_target_pairs={{0,64},{32,96},{64,128},{96,160},{128,192},{160,224},{192,0},{224,... | collective-permute-start | bytes 393224 | tf_op jit(solution)/shard_map/ppermute | solution.py:245
  117.1 2.5 %collective-permute-done.6.refs_6_ = bf16[128,512]{1,0:T(8,128)(2,1)S(1)} collective-permute-done((bf16[128,512]{1,0:T(8,128)(2,1)S(1)}, bf16[128,512]{1,0:T(8,128)(2,1)S(1)}, u32[]{:S(2)}, u32[]{:S(2)}) %collective-permute-start.6) | collective-permute-done | bytes 131104 | tf_op jit(solution)/shard_map/ppermute | solution.py:245
  119.6 1.8 %collective-permute-done.5.refs_5_ = bf16[128,512]{1,0:T(8,128)(2,1)S(1)} collective-permute-done((bf16[128,512]{1,0:T(8,128)(2,1)S(1)}, bf16[128,512]{1,0:T(8,128)(2,1)S(1)}, u32[]{:S(2)}, u32[]{:S(2)}) %collective-permute-start.5) | collective-permute-done | bytes 131104 | tf_op jit(solution)/shard_map/ppermute | solution.py:245
  121.4 11.3 %collective-permute-done.3.refs_3_ = bf16[128,512]{1,0:T(8,128)(2,1)S(1)} collective-permute-done((bf16[128,512]{1,0:T(8,128)(2,1)S(1)}, bf16[128,512]{1,0:T(8,128)(2,1)S(1)}, u32[]{:S(2)}, u32[]{:S(2)}) %collective-permute-start.3) | collective-permute-done | bytes 131104 | tf_op jit(solution)/shard_map/ppermute | solution.py:245
  132.8 5.0 %collective-permute-done.1.refs_1_ = bf16[128,512]{1,0:T(8,128)(2,1)S(1)} collective-permute-done((bf16[128,512]{1,0:T(8,128)(2,1)S(1)}, bf16[128,512]{1,0:T(8,128)(2,1)S(1)}, u32[]{:S(2)}, u32[]{:S(2)}) %collective-permute-start.1) | collective-permute-done | bytes 131104 | tf_op jit(solution)/shard_map/ppermute | solution.py:245
  137.8 1.4 %gate.1 = bf16[1024,512]{1,0:T(8,128)(2,1)} custom-call(s32[1]{0:T(128)} %bitcast.here_ref, bf16[128,512]{1,0:T(8,128)(2,1)S(1)} %get-tuple-element.20.refs_0_, bf16[128,512]{1,0:T(8,128)(2,1)S(1)} %collective-permute-done.1.refs_1_, bf16[128,512]{1,0:T(8,128)(2,1)S(1)} %collective-permute-done.2.refs_2_, ...), custom_call_target="tpu_custom_call" | custom-call | flops 1048576 | bytes 3145728 | tf_op jit(solution)/shard_map/gate/pallas_call | solution.py:208
  (17 shorter events, 1.1 us)
Async XLA Ops:
  1.4 27.3 %all-to-all-start = ((bf16[32,8,128]{2,1,0:T(8,128)(2,1)}), bf16[32,8,128]{2,1,0:T(8,128)(2,1)S(1)}, u32[]{:S(2)}, u32[]{:S(2)}) async-start(bf16[32,8,128]{2,1,0:T(8,128)(2,1)} %bitcast.18), calls=%async_computation | async-start | bytes 131072 | tf_op jit(solution)/shard_map/all_to_all | solution.py:236
  10.9 9.5 %collective-permute-start = (bf16[3,2,4096]{2,1,0:T(2,128)(2,1)S(1)}, bf16[3,2,4096]{2,1,0:T(2,128)(2,1)S(1)}, u32[]{:S(2)}, u32[]{:S(2)}) collective-permute-start(bf16[3,2,4096]{2,1,0:T(2,128)(2,1)S(1)} %slice.36), channel_id=1, source_target_pairs={{0,32},{32,64},{64,96},{96,128},{128,160},{160,192},{192,224},{224... | collective-permute-start | bytes 147464 | tf_op jit(solution)/shard_map/ppermute | solution.py:231
  20.4 0.6 copy-start.3
  28.6 12.9 %copy-start.2 = (bf16[32,8,128]{2,1,0:T(8,128)(2,1)}, bf16[32,8,128]{2,1,0:T(8,128)(2,1)S(1)}, u32[]{:S(2)}) copy-start(bf16[32,8,128]{2,1,0:T(8,128)(2,1)S(1)} %all-to-all-done) | copy-start | bytes 196612
  28.6 42.6 %all-to-all-start.1 = ((bf16[256,16,128]{2,1,0:T(8,128)(2,1)}), bf16[256,16,128]{2,1,0:T(8,128)(2,1)S(1)}, u32[]{:S(2)}, u32[]{:S(2)}) async-start(bf16[256,16,128]{2,1,0:T(8,128)(2,1)} %get-tuple-element.11), calls=%async_computation.1 | async-start | bytes 2097152 | tf_op jit(solution)/shard_map/all_to_all | solution.py:241
  71.2 1.1 copy-start.1
  72.3 34.3 %copy-start = (bf16[8,128,512]{2,1,0:T(8,128)(2,1)S(1)}, bf16[8,128,512]{2,1,0:T(8,128)(2,1)}, u32[]{:S(2)}) copy-start(bf16[8,128,512]{2,1,0:T(8,128)(2,1)} %get-tuple-element.9) | copy-start | bytes 3145732
  101.0 36.8 %all-to-all-start.2 = ((bf16[32,8,16,128]{3,2,1,0:T(8,128)(2,1)}), bf16[32,8,16,128]{3,2,1,0:T(8,128)(2,1)S(1)}, u32[]{:S(2)}, u32[]{:S(2)}) async-start(bf16[32,8,16,128]{3,2,1,0:T(8,128)(2,1)} %bitcast.30), calls=%async_computation.2 | async-start | bytes 2097152 | tf_op jit(solution)/shard_map/all_to_all | solution.py:251
  106.7 8.6 %collective-permute-start.7 = (bf16[128,512]{1,0:T(8,128)(2,1)S(1)}, bf16[128,512]{1,0:T(8,128)(2,1)S(1)}, u32[]{:S(2)}, u32[]{:S(2)}) collective-permute-start(bf16[128,512]{1,0:T(8,128)(2,1)S(1)} %get-tuple-element.13), channel_id=1, source_target_pairs={{0,224},{32,0},{64,32},{96,64},{128,96},{160,128},{192,160},{224,1... | collective-permute-start | bytes 393224 | tf_op jit(solution)/shard_map/ppermute | solution.py:245
  107.9 11.7 %collective-permute-start.6 = (bf16[128,512]{1,0:T(8,128)(2,1)S(1)}, bf16[128,512]{1,0:T(8,128)(2,1)S(1)}, u32[]{:S(2)}, u32[]{:S(2)}) collective-permute-start(bf16[128,512]{1,0:T(8,128)(2,1)S(1)} %get-tuple-element.14), channel_id=1, source_target_pairs={{0,192},{32,224},{64,0},{96,32},{128,64},{160,96},{192,128},{224,1... | collective-permute-start | bytes 393224 | tf_op jit(solution)/shard_map/ppermute | solution.py:245
  107.9 13.5 %collective-permute-start.5 = (bf16[128,512]{1,0:T(8,128)(2,1)S(1)}, bf16[128,512]{1,0:T(8,128)(2,1)S(1)}, u32[]{:S(2)}, u32[]{:S(2)}) collective-permute-start(bf16[128,512]{1,0:T(8,128)(2,1)S(1)} %get-tuple-element.15), channel_id=1, source_target_pairs={{0,160},{32,192},{64,224},{96,0},{128,32},{160,64},{192,96},{224,1... | collective-permute-start | bytes 393224 | tf_op jit(solution)/shard_map/ppermute | solution.py:245
  110.8 10.7 %collective-permute-start.4 = (bf16[128,512]{1,0:T(8,128)(2,1)S(1)}, bf16[128,512]{1,0:T(8,128)(2,1)S(1)}, u32[]{:S(2)}, u32[]{:S(2)}) collective-permute-start(bf16[128,512]{1,0:T(8,128)(2,1)S(1)} %get-tuple-element.16), channel_id=1, source_target_pairs={{0,128},{32,160},{64,192},{96,224},{128,0},{160,32},{192,64},{224,... | collective-permute-start | bytes 393224 | tf_op jit(solution)/shard_map/ppermute | solution.py:245
  113.4 19.4 %collective-permute-start.3 = (bf16[128,512]{1,0:T(8,128)(2,1)S(1)}, bf16[128,512]{1,0:T(8,128)(2,1)S(1)}, u32[]{:S(2)}, u32[]{:S(2)}) collective-permute-start(bf16[128,512]{1,0:T(8,128)(2,1)S(1)} %get-tuple-element.17), channel_id=1, source_target_pairs={{0,96},{32,128},{64,160},{96,192},{128,224},{160,0},{192,32},{224,... | collective-permute-start | bytes 393224 | tf_op jit(solution)/shard_map/ppermute | solution.py:245
  115.4 17.4 %collective-permute-start.2 = (bf16[128,512]{1,0:T(8,128)(2,1)S(1)}, bf16[128,512]{1,0:T(8,128)(2,1)S(1)}, u32[]{:S(2)}, u32[]{:S(2)}) collective-permute-start(bf16[128,512]{1,0:T(8,128)(2,1)S(1)} %get-tuple-element.18), channel_id=1, source_target_pairs={{0,64},{32,96},{64,128},{96,160},{128,192},{160,224},{192,0},{224,... | collective-permute-start | bytes 393224 | tf_op jit(solution)/shard_map/ppermute | solution.py:245
  119.6 18.1 %collective-permute-start.1 = (bf16[128,512]{1,0:T(8,128)(2,1)S(1)}, bf16[128,512]{1,0:T(8,128)(2,1)S(1)}, u32[]{:S(2)}, u32[]{:S(2)}) collective-permute-start(bf16[128,512]{1,0:T(8,128)(2,1)S(1)} %get-tuple-element.19), channel_id=1, source_target_pairs={{0,32},{32,64},{64,96},{96,128},{128,160},{160,192},{192,224},{224... | collective-permute-start | bytes 393224 | tf_op jit(solution)/shard_map/ppermute | solution.py:245

commit v3 on v2

v3 whole, which is shorter than its diff:
```python
import jax
import jax.numpy as jnp
from jax import lax
from jax.experimental import pallas as pl
from jax.experimental.pallas import tpu as pltpu
from jax.sharding import PartitionSpec as P


F32 = jnp.float32
BF16 = jnp.bfloat16
TILE = 128
ROW_CHUNK = 512
SPLIT = 4
MIB = 1024 * 1024
SMALL = pltpu.CompilerParams(vmem_limit_bytes=16 * MIB)
LARGE = pltpu.CompilerParams(vmem_limit_bytes=58 * MIB)
WIDE = pltpu.CompilerParams(vmem_limit_bytes=62 * MIB)
WHOLE = pl.BlockSpec(memory_space=pltpu.VMEM)
FAR = pl.BlockSpec(memory_space=pltpu.HBM)
SCALARS = pl.BlockSpec(memory_space=pltpu.SMEM)


def estimate(flops, moved):
    return pl.CostEstimate(flops=flops, bytes_accessed=moved, transcendentals=0)


def identity(size):
    rows = lax.broadcasted_iota(jnp.int32, (size, size), 0)
    return (rows == lax.broadcasted_iota(jnp.int32, (size, size), 1)).astype(BF16)


def transposed(value, ones):
    return lax.dot_general(ones, value, (((1,), (1,)), ((), ())), preferred_element_type=F32)


def featurize_kernel(
    here_ref, own_ref, before_ref, taps_ref, query_ref, kv_ref, x_ref, rows_ref, made_ref, sent_ref, arrived, left
):
    taps, streams, _ = taps_ref.shape
    slots, rows, columns = made_ref.shape
    pieces, per_device = sent_ref.shape[1:3]
    lead = rows_ref.shape[1] - rows
    parts = columns // TILE
    count = TILE // per_device
    earlier = taps - 1
    ones = identity(TILE)

    def fetch(which):
        return pltpu.make_async_copy(own_ref.at[which], x_ref.at[which], arrived.at[which])

    def leave(slot):
        turn = (slot + slots - here_ref[0]) % slots
        first = pl.multiple_of(slot * pieces, pieces)
        return (
            pltpu.make_async_copy(made_ref.at[slot], query_ref.at[turn], left.at[0, slot]),
            pltpu.make_async_copy(
                sent_ref.at[slot], kv_ref.at[pl.ds(first, pieces)], left.at[1, slot]
            ),
        )

    for which in range(streams):
        fetch(which).start()
    for which in range(streams):
        fetch(which).wait()

    def step(slot, carry):
        for part in range(parts):
            lanes = slice(part * TILE, (part + 1) * TILE)
            along = pl.ds(pl.multiple_of(slot * columns + part * TILE, TILE), TILE)

            def feature(which):
                slab = which * parts + part
                rows_ref[slab, lead:, :] = x_ref[which, :, along].astype(F32)
                rows_ref[slab, lead - earlier : lead, :] = before_ref[which, :, along].astype(F32)
                weights = taps_ref[:, which, along].astype(F32)
                total = weights[0:1] * rows_ref[slab, lead:, :]
                for lag in range(1, taps):
                    moved = rows_ref[slab, lead - lag : lead - lag + rows, :]
                    total = total + weights[lag : lag + 1] * moved
                return total

            made_ref[slot, :, lanes] = feature(0).astype(BF16)
            product = (feature(1) * feature(2)).astype(BF16)
            turned = transposed(product, ones).astype(BF16)
            sent_ref[slot, part * count : (part + 1) * count] = turned.reshape(
                count, per_device, rows
            )
        for copy in leave(slot):
            copy.start()
        return carry

    lax.fori_loop(0, slots, step, 0)
    for slot in range(slots):
        for copy in leave(slot):
            copy.wait()


def featurize(here, own, before, taps, slots, per_device):
    streams, rows, channels = own.shape
    columns = channels // slots
    pieces = columns // per_device
    return pl.pallas_call(
        featurize_kernel,
        out_shape=(
            jax.ShapeDtypeStruct((slots, rows, columns), BF16),
            jax.ShapeDtypeStruct((slots * pieces, per_device, rows), BF16),
        ),
        in_specs=[SCALARS, FAR, WHOLE, WHOLE],
        out_specs=(FAR, FAR),
        scratch_shapes=[
            pltpu.VMEM((streams, rows, channels), BF16),
            pltpu.VMEM((streams * columns // TILE, rows + 8, TILE), F32),
            pltpu.VMEM((slots, rows, columns), BF16),
            pltpu.VMEM((slots, pieces, per_device, rows), BF16),
            pltpu.SemaphoreType.DMA((streams,)),
            pltpu.SemaphoreType.DMA((2, slots)),
        ],
        compiler_params=WIDE,
        cost_estimate=estimate(20 * own.size, 4 * own.size),
        name="featurize",
    )(here, own, before, taps)


def toeplitz_kernel(lags_ref, out_ref, earlier_ref):
    count, tile = lags_ref.shape
    upper = lax.broadcasted_iota(jnp.int32, (tile, tile), 1) >= lax.broadcasted_iota(
        jnp.int32, (tile, tile), 0
    )

    @pl.when(pl.program_id(0) == 0)
    def _():
        earlier_ref[...] = jnp.zeros_like(earlier_ref)

    earlier = earlier_ref[...]
    lines = lags_ref[...].astype(F32)
    for part in range(count):
        spread = jnp.broadcast_to(lines[part : part + 1], (tile, tile))
        turned = pltpu.roll(spread, 0, 1, stride=1, stride_axis=0)
        place = slice(part * tile, (part + 1) * tile)
        out_ref[place, :] = jnp.where(upper, turned, earlier).astype(BF16)
        earlier = turned
    earlier_ref[...] = earlier


def toeplitz(lags):
    count, tile = lags.shape
    each = 16
    return pl.pallas_call(
        toeplitz_kernel,
        grid=(count // each,),
        out_shape=jax.ShapeDtypeStruct((count * tile, tile), BF16),
        in_specs=[pl.BlockSpec((each, tile), lambda i: (i, 0))],
        out_specs=pl.BlockSpec((each * tile, tile), lambda i: (i, 0)),
        scratch_shapes=[pltpu.VMEM((tile, tile), F32)],
        compiler_params=WIDE,
        cost_estimate=estimate(4 * count * tile * tile, 2 * count * tile * tile),
        name="toeplitz",
    )(lags)


def convolve_kernel(
    here_ref, gain_ref, x_ref, tiles_ref, out_ref, weights_ref, pair_ref, total_ref, made_ref, arrived, left
):
    slots, devices, channels, tile = x_ref.shape
    pairs = slots * devices // 2
    group = ROW_CHUNK // channels
    share = 2 * group * tile // SPLIT

    def fetch(index, piece):
        start = pl.multiple_of((index * SPLIT + piece) * share, share)
        kept = pl.multiple_of(start + tile, tile)
        return pltpu.make_async_copy(
            tiles_ref.at[pl.ds(start, share), :],
            weights_ref.at[pl.ds(kept, share), :],
            arrived.at[index, piece],
        )

    def leave(index):
        first = pl.ds(pl.multiple_of(index * (2 * group), 2 * group), 2 * group)
        return pltpu.make_async_copy(made_ref.at[first], out_ref.at[first], left.at[index])

    shares = pairs // group
    for piece in range(SPLIT):
        fetch(0, piece).start()
    weights_ref[0:tile, :] = jnp.zeros((tile, tile), BF16)
    part = group // SPLIT
    margin = part * channels
    pair_ref[0:margin, :] = jnp.zeros((margin, 2 * tile), BF16)
    for pair in range(pairs):
        start = margin + pair * channels
        for half in range(2):
            block = 2 * pair + 1 - half
            lanes = slice(half * tile, (half + 1) * tile)
            pair_ref[start : start + channels, lanes] = x_ref[block % slots, block // slots]
    channel = lax.broadcasted_iota(jnp.int32, (channels, tile), 0)
    gain = jnp.zeros((channels, tile), F32)
    for index in range(channels):
        gain = jnp.where(channel == index, gain_ref[here_ref[0] * channels + index], gain)

    def product(lag, count, starts, height):
        base = pl.multiple_of(lag * (2 * tile), 2 * tile)
        next_base = pl.multiple_of(base + tile, tile)
        depth = count * 2 * tile
        weights = jnp.concatenate(
            [weights_ref[pl.ds(base, depth), :], weights_ref[pl.ds(next_base, depth), :]], axis=1
        )
        rows = jnp.concatenate([pair_ref[pl.ds(start, height), :] for start in starts], axis=1)
        return jnp.dot(rows, weights, preferred_element_type=F32)

    def chunk(index, carry):
        for piece in range(SPLIT):
            fetch(index, piece).wait()

        @pl.when(index + 1 < shares)
        def _():
            for piece in range(SPLIT):
                fetch(index + 1, piece).start()

        top = pl.multiple_of(index * ROW_CHUNK, ROW_CHUNK)
        for piece in range(SPLIT):
            skipped = piece * margin
            starts = [margin - i * channels for i in range(part)]
            lag = index * group + piece * part
            value = product(lag, part, starts, ROW_CHUNK - skipped)
            if piece == 0:
                total_ref[...] = value
            else:
                total_ref[skipped:, :] += value

        def step(past, inner):
            first = margin + top - past * ROW_CHUNK
            starts = [pl.multiple_of(first - i * channels, channels) for i in range(group)]
            total_ref[...] += product(past * group, group, starts, ROW_CHUNK)
            return inner

        lax.fori_loop(0, index, step, 0)
        for pair in range(group):
            rows = slice(pair * channels, (pair + 1) * channels)
            for half in range(2):
                block = 2 * pair + half
                lanes = slice(half * tile, (half + 1) * tile)
                device = index * (2 * group // slots) + block // slots
                direct = gain * x_ref[block % slots, device].astype(F32)
                made_ref[index * (2 * group) + block] = (total_ref[rows, lanes] + direct).astype(BF16)
        leave(index).start()
        return carry

    lax.fori_loop(0, shares, chunk, 0)
    for index in range(shares):
        leave(index).wait()


def convolve(here, gain, x, weights):
    slots, devices, channels, tile = x.shape
    blocks = slots * devices
    height = blocks // 2 * channels
    return pl.pallas_call(
        convolve_kernel,
        out_shape=jax.ShapeDtypeStruct((blocks, channels, tile), BF16),
        in_specs=[SCALARS, SCALARS, WHOLE, FAR],
        out_specs=FAR,
        scratch_shapes=[
            pltpu.VMEM((weights.shape[0] + tile, tile), BF16),
            pltpu.VMEM((height + ROW_CHUNK // SPLIT, 2 * tile), BF16),
            pltpu.VMEM((ROW_CHUNK, 2 * tile), F32),
            pltpu.VMEM((blocks, channels, tile), BF16),
            pltpu.SemaphoreType.DMA((height // ROW_CHUNK, SPLIT)),
            pltpu.SemaphoreType.DMA((height // ROW_CHUNK,)),
        ],
        compiler_params=LARGE,
        cost_estimate=estimate(blocks * blocks * channels * tile * tile, 4 * x.size + 2 * weights.size),
        name="convolve",
    )(here, gain, x, weights)


def gate_kernel(here_ref, *refs):
    queries, mixed_ref, out_ref = refs[:-2], refs[-2], refs[-1]
    slots = len(queries)
    rows, columns = queries[0].shape
    ones = identity(rows)
    for shift, query_ref in enumerate(queries):
        slot = (here_ref[0] + slots - shift) % slots
        mixed = mixed_ref[:, pl.ds(slot, 1)].reshape(columns, rows)
        target = pl.ds(pl.multiple_of(slot * rows, rows), rows)
        out_ref[target, :] = (query_ref[...].astype(F32) * transposed(mixed, ones)).astype(BF16)


def gate(here, queries, mixed):
    rows, columns = queries[0].shape
    total = len(queries) * rows
    return pl.pallas_call(
        gate_kernel,
        out_shape=jax.ShapeDtypeStruct((total, columns), BF16),
        in_specs=[SCALARS] + [WHOLE] * (len(queries) + 1),
        out_specs=WHOLE,
        compiler_params=SMALL,
        cost_estimate=estimate(2 * total * columns, 6 * total * columns),
        name="gate",
    )(here, *queries, mixed)


def stages(projected, short_taps, long_filter, skip_gain):
    devices = lax.axis_size("ctx")
    slots = lax.axis_size("chan")
    own = jnp.transpose(projected[0], (1, 0, 2))
    rows = own.shape[1]
    columns = skip_gain.shape[0]
    channels = columns // devices
    lags = short_taps.shape[0]
    here = lax.axis_index("chan").astype(jnp.int32).reshape(1)

    order = [(t % slots) * devices + t // slots for t in range(slots * devices)]
    pairs = list(zip(order, order[1:]))
    before = lax.ppermute(own[:, rows - (lags - 1) :], ("chan", "ctx"), pairs)

    groups = long_filter.shape[1]
    lines = jnp.repeat(long_filter.T.astype(BF16), devices // groups, axis=0)
    lines = lines.reshape(devices, -1, TILE)
    lines = lax.all_to_all(lines, "ctx", 0, 0, tiled=True).reshape(-1, TILE)

    query, kv = featurize(here, own, before, short_taps, slots, channels)
    lines, kv = lax.optimization_barrier((lines, kv))
    weights = toeplitz(lines)
    kv = lax.all_to_all(kv, ("chan", "ctx"), 0, 0, tiled=True)
    queries = [query[0]]
    for shift in range(1, slots):
        ring = [(i, (i + shift) % slots) for i in range(slots)]
        queries.append(lax.ppermute(query[shift], "chan", ring))

    place = lax.axis_index("ctx").astype(jnp.int32).reshape(1)
    kv = kv.reshape(slots, devices, channels, rows)
    mixed = convolve(place, skip_gain, kv, weights)
    mixed = mixed.reshape(devices, slots, channels, rows)
    mixed = lax.all_to_all(mixed, "ctx", 0, 0, tiled=True)
    return gate(here, queries, mixed)


def solution(mesh):
    placed = (P("ctx", "chan", None, None), P(), P("ctx", "chan"), P("chan"))
    return jax.shard_map(
        stages, mesh=mesh, in_specs=placed, out_specs=P("ctx", "chan"), check_vma=False
    )
```

time: 140 us -> 135 us (0.964)
  Pallas kernels: 46.8 us -> 42.9 us
    pallas_call x3, Pallas kernels: 45.4 us -> 41.4 us  [the longest x1 24.2 us: convolve(): pl.pallas_call(convolve_kernel, out_shape=jax.ShapeDtypeStruct((blocks, c...]
  transfers between devices with their start and end apart: 11 -> 11, of which waited for: 6 -> 6; matrix products, arithmetic and copies ran while one was open for 1% -> 1% of each run, Pallas kernels for 12% -> 13%
where the time goes in v3:
time: 135 us; the launch traced here: 134 us
  waiting for transfers between devices  46.7 us (35%)
  Pallas kernels  42.9 us (32%)
  starting transfers between devices  40.3 us (30%)
  local copies, waits for them, and re-layouts  3.42 us (3%)
    pallas_call x1, Pallas kernels, convolve(): pl.pallas_call(convolve_kernel, out_shape=jax.ShapeDtypeStruct((blocks, c...  24.2 us
    ppermute x7, waiting for transfers between devices, stages(): queries.append(lax.ppermute(query[shift], 'chan', ring))  20.7 us
    all_to_all x1, waiting for transfers between devices, stages(): kv = lax.all_to_all(kv, ('chan', 'ctx'), 0, 0, tiled=True)  20.1 us
    all_to_all x1, starting transfers between devices, stages(): kv = lax.all_to_all(kv, ('chan', 'ctx'), 0, 0, tiled=True)  12.2 us
    ppermute x7, starting transfers between devices, stages(): queries.append(lax.ppermute(query[shift], 'chan', ring))  10.3 us
    pallas_call x1, Pallas kernels, toeplitz(): pl.pallas_call(toeplitz_kernel, grid=(count // each,), out_shape=jax.Shap...  10.3 us
    all_to_all x1, starting transfers between devices, stages(): lines = lax.all_to_all(lines, 'ctx', 0, 0, tiled=True).reshape(-1, TILE)  8.58 us
    pallas_call x1, Pallas kernels, featurize(): pl.pallas_call(featurize_kernel, out_shape=(jax.ShapeDtypeStruct((slots,...  6.95 us
  transfers between devices with their start and end apart: 11, of which 6 were waited for; matrix products, arithmetic and copies ran while one was open for 1% of the time, Pallas kernels for 13%

profile of v3, /device:TPU:1, one launch (start us, length us, event | category | flops | bytes accessed | tf_op | source)
XLA Modules:
  0.0 134.1 jit_solution(17425908564631584590)
XLA Ops:
  0.0 0.7 convert_bitcast_fusion
  0.7 0.6 copy.5
  1.4 8.6 %all-to-all-start = ((bf16[32,8,128]{2,1,0:T(8,128)(2,1)}), bf16[32,8,128]{2,1,0:T(8,128)(2,1)S(1)}, u32[]{:S(2)}, u32[]{:S(2)}) async-start(bf16[32,8,128]{2,1,0:T(8,128)(2,1)} %bitcast.19), calls=%async_computation | async-start | bytes 131072 | tf_op jit(solution)/shard_map/all_to_all | solution.py:319
  9.9 1.0 slice.36
  10.9 3.5 %collective-permute-start = (bf16[3,2,4096]{2,1,0:T(2,128)(2,1)S(1)}, bf16[3,2,4096]{2,1,0:T(2,128)(2,1)S(1)}, u32[]{:S(2)}, u32[]{:S(2)}) collective-permute-start(bf16[3,2,4096]{2,1,0:T(2,128)(2,1)S(1)} %slice.36), channel_id=1, source_target_pairs={{0,32},{32,64},{64,96},{96,128},{128,160},{160,192},{192,224},{224... | collective-permute-start | bytes 147464 | tf_op jit(solution)/shard_map/ppermute | solution.py:314
  14.5 5.9 %collective-permute-done.before_ref = bf16[3,2,4096]{2,1,0:T(2,128)(2,1)S(1)} collective-permute-done((bf16[3,2,4096]{2,1,0:T(2,128)(2,1)S(1)}, bf16[3,2,4096]{2,1,0:T(2,128)(2,1)S(1)}, u32[]{:S(2)}, u32[]{:S(2)}) %collective-permute-start) | collective-permute-done | bytes 49184 | tf_op jit(solution)/shard_map/ppermute | solution.py:314
  20.4 0.6 copy-done.3
  21.0 7.0 %featurize.1 = (bf16[8,128,512]{2,1,0:T(8,128)(2,1)}, bf16[256,16,128]{2,1,0:T(8,128)(2,1)}) custom-call(s32[1]{0:T(128)} %bitcast.here_ref, bf16[3,128,4096]{2,1,0:T(8,128)(2,1)} %bitcast.30, bf16[3,2,4096]{2,1,0:T(2,128)(2,1)} %copy-done.3, bf16[3,3,4096]{2,1,0:T(4,128)(2,1)} %taps_ref.1), custom_call_target="tpu_custom_call" | custom-call | flops 31457280 | bytes 6291456 | tf_op jit(solution)/shard_map/featurize/pallas_call | solution.py:102
  28.0 12.2 %all-to-all-start.1 = ((bf16[256,16,128]{2,1,0:T(8,128)(2,1)}), bf16[256,16,128]{2,1,0:T(8,128)(2,1)S(1)}, u32[]{:S(2)}, u32[]{:S(2)}) async-start(bf16[256,16,128]{2,1,0:T(8,128)(2,1)} %get-tuple-element.11), calls=%async_computation.1 | async-start | bytes 2097152 | tf_op jit(solution)/shard_map/all_to_all | solution.py:324
  40.2 10.3 %toeplitz.1.tiles_ref = bf16[32768,128]{1,0:T(8,128)(2,1)} custom-call(bf16[256,128]{1,0:T(8,128)(2,1)} %bitcast.33), custom_call_target="tpu_custom_call" | custom-call | flops 16777216 | bytes 8388608 | tf_op jit(solution)/shard_map/toeplitz/pallas_call | solution.py:148
  50.5 20.1 %all-to-all-done.1 = bf16[256,16,128]{2,1,0:T(8,128)(2,1)S(1)} async-done(((bf16[256,16,128]{2,1,0:T(8,128)(2,1)}), bf16[256,16,128]{2,1,0:T(8,128)(2,1)S(1)}, u32[]{:S(2)}, u32[]{:S(2)}) %all-to-all-start.1) | async-done | bytes 1048608 | tf_op jit(solution)/shard_map/all_to_all | solution.py:324
  70.6 1.1 copy-done.1
  71.6 24.2 %convolve.1 = bf16[256,16,128]{2,1,0:T(8,128)(2,1)} custom-call(s32[1]{0:T(128)} %bitcast.12.here_ref, f32[512]{0:T(512)} %gain_ref.1, bf16[8,32,16,128]{3,2,1,0:T(8,128)(2,1)} %bitcast.32, bf16[32768,128]{1,0:T(8,128)(2,1)} %toeplitz.1.tiles_ref), custom_call_target="tpu_custom_call" | custom-call | flops 17179869184 | bytes 10485760 | tf_op jit(solution)/shard_map/convolve/pallas_call | solution.py:257
  95.9 5.6 %all-to-all-start.2 = ((bf16[32,8,16,128]{3,2,1,0:T(8,128)(2,1)}), bf16[32,8,16,128]{3,2,1,0:T(8,128)(2,1)S(1)}, u32[]{:S(2)}, u32[]{:S(2)}) async-start(bf16[32,8,16,128]{3,2,1,0:T(8,128)(2,1)} %bitcast.31), calls=%async_computation.2 | async-start | bytes 2097152 | tf_op jit(solution)/shard_map/all_to_all | solution.py:334
  101.6 1.2 collective-permute-start.7
  102.8 2.9 %collective-permute-start.5 = (bf16[128,512]{1,0:T(8,128)(2,1)S(1)}, bf16[128,512]{1,0:T(8,128)(2,1)S(1)}, u32[]{:S(2)}, u32[]{:S(2)}) collective-permute-start(bf16[128,512]{1,0:T(8,128)(2,1)S(1)} %get-tuple-element.15), channel_id=1, source_target_pairs={{0,160},{32,192},{64,224},{96,0},{128,32},{160,64},{192,96},{224,1... | collective-permute-start | bytes 393224 | tf_op jit(solution)/shard_map/ppermute | solution.py:328
  105.7 2.6 %collective-permute-start.4 = (bf16[128,512]{1,0:T(8,128)(2,1)S(1)}, bf16[128,512]{1,0:T(8,128)(2,1)S(1)}, u32[]{:S(2)}, u32[]{:S(2)}) collective-permute-start(bf16[128,512]{1,0:T(8,128)(2,1)S(1)} %get-tuple-element.16), channel_id=1, source_target_pairs={{0,128},{32,160},{64,192},{96,224},{128,0},{160,32},{192,64},{224,... | collective-permute-start | bytes 393224 | tf_op jit(solution)/shard_map/ppermute | solution.py:328
  108.3 2.0 %collective-permute-start.3 = (bf16[128,512]{1,0:T(8,128)(2,1)S(1)}, bf16[128,512]{1,0:T(8,128)(2,1)S(1)}, u32[]{:S(2)}, u32[]{:S(2)}) collective-permute-start(bf16[128,512]{1,0:T(8,128)(2,1)S(1)} %get-tuple-element.17), channel_id=1, source_target_pairs={{0,96},{32,128},{64,160},{96,192},{128,224},{160,0},{192,32},{224,... | collective-permute-start | bytes 393224 | tf_op jit(solution)/shard_map/ppermute | solution.py:328
  110.3 1.7 %collective-permute-start.2 = (bf16[128,512]{1,0:T(8,128)(2,1)S(1)}, bf16[128,512]{1,0:T(8,128)(2,1)S(1)}, u32[]{:S(2)}, u32[]{:S(2)}) collective-permute-start(bf16[128,512]{1,0:T(8,128)(2,1)S(1)} %get-tuple-element.18), channel_id=1, source_target_pairs={{0,64},{32,96},{64,128},{96,160},{128,192},{160,224},{192,0},{224,... | collective-permute-start | bytes 393224 | tf_op jit(solution)/shard_map/ppermute | solution.py:328
  112.0 2.6 %collective-permute-done.6.refs_6_ = bf16[128,512]{1,0:T(8,128)(2,1)S(1)} collective-permute-done((bf16[128,512]{1,0:T(8,128)(2,1)S(1)}, bf16[128,512]{1,0:T(8,128)(2,1)S(1)}, u32[]{:S(2)}, u32[]{:S(2)}) %collective-permute-start.6) | collective-permute-done | bytes 131104 | tf_op jit(solution)/shard_map/ppermute | solution.py:328
  114.5 1.8 %collective-permute-done.5.refs_5_ = bf16[128,512]{1,0:T(8,128)(2,1)S(1)} collective-permute-done((bf16[128,512]{1,0:T(8,128)(2,1)S(1)}, bf16[128,512]{1,0:T(8,128)(2,1)S(1)}, u32[]{:S(2)}, u32[]{:S(2)}) %collective-permute-start.5) | collective-permute-done | bytes 131104 | tf_op jit(solution)/shard_map/ppermute | solution.py:328
  116.3 11.3 %collective-permute-done.3.refs_3_ = bf16[128,512]{1,0:T(8,128)(2,1)S(1)} collective-permute-done((bf16[128,512]{1,0:T(8,128)(2,1)S(1)}, bf16[128,512]{1,0:T(8,128)(2,1)S(1)}, u32[]{:S(2)}, u32[]{:S(2)}) %collective-permute-start.3) | collective-permute-done | bytes 131104 | tf_op jit(solution)/shard_map/ppermute | solution.py:328
  127.7 5.0 %collective-permute-done.1.refs_1_ = bf16[128,512]{1,0:T(8,128)(2,1)S(1)} collective-permute-done((bf16[128,512]{1,0:T(8,128)(2,1)S(1)}, bf16[128,512]{1,0:T(8,128)(2,1)S(1)}, u32[]{:S(2)}, u32[]{:S(2)}) %collective-permute-start.1) | collective-permute-done | bytes 131104 | tf_op jit(solution)/shard_map/ppermute | solution.py:328
  132.7 1.4 %gate.1 = bf16[1024,512]{1,0:T(8,128)(2,1)} custom-call(s32[1]{0:T(128)} %bitcast.here_ref, bf16[128,512]{1,0:T(8,128)(2,1)S(1)} %get-tuple-element.20.refs_0_, bf16[128,512]{1,0:T(8,128)(2,1)S(1)} %collective-permute-done.1.refs_1_, bf16[128,512]{1,0:T(8,128)(2,1)S(1)} %collective-permute-done.2.refs_2_, ...), custom_call_target="tpu_custom_call" | custom-call | flops 1048576 | bytes 3145728 | tf_op jit(solution)/shard_map/gate/pallas_call | solution.py:291
  (15 shorter events, 0.1 us)
Async XLA Ops:
  1.4 26.6 %all-to-all-start = ((bf16[32,8,128]{2,1,0:T(8,128)(2,1)}), bf16[32,8,128]{2,1,0:T(8,128)(2,1)S(1)}, u32[]{:S(2)}, u32[]{:S(2)}) async-start(bf16[32,8,128]{2,1,0:T(8,128)(2,1)} %bitcast.19), calls=%async_computation | async-start | bytes 131072 | tf_op jit(solution)/shard_map/all_to_all | solution.py:319
  10.9 9.5 %collective-permute-start = (bf16[3,2,4096]{2,1,0:T(2,128)(2,1)S(1)}, bf16[3,2,4096]{2,1,0:T(2,128)(2,1)S(1)}, u32[]{:S(2)}, u32[]{:S(2)}) collective-permute-start(bf16[3,2,4096]{2,1,0:T(2,128)(2,1)S(1)} %slice.36), channel_id=1, source_target_pairs={{0,32},{32,64},{64,96},{96,128},{128,160},{160,192},{192,224},{224... | collective-permute-start | bytes 147464 | tf_op jit(solution)/shard_map/ppermute | solution.py:314
  20.4 0.6 copy-start.3
  28.0 12.2 %copy-start.2 = (bf16[32,8,128]{2,1,0:T(8,128)(2,1)}, bf16[32,8,128]{2,1,0:T(8,128)(2,1)S(1)}, u32[]{:S(2)}) copy-start(bf16[32,8,128]{2,1,0:T(8,128)(2,1)S(1)} %all-to-all-done) | copy-start | bytes 196612
  28.0 42.6 %all-to-all-start.1 = ((bf16[256,16,128]{2,1,0:T(8,128)(2,1)}), bf16[256,16,128]{2,1,0:T(8,128)(2,1)S(1)}, u32[]{:S(2)}, u32[]{:S(2)}) async-start(bf16[256,16,128]{2,1,0:T(8,128)(2,1)} %get-tuple-element.11), calls=%async_computation.1 | async-start | bytes 2097152 | tf_op jit(solution)/shard_map/all_to_all | solution.py:324
  70.6 1.1 copy-start.1
  71.6 29.9 %copy-start = (bf16[8,128,512]{2,1,0:T(8,128)(2,1)S(1)}, bf16[8,128,512]{2,1,0:T(8,128)(2,1)}, u32[]{:S(2)}) copy-start(bf16[8,128,512]{2,1,0:T(8,128)(2,1)} %get-tuple-element.9) | copy-start | bytes 3145732
  95.9 36.8 %all-to-all-start.2 = ((bf16[32,8,16,128]{3,2,1,0:T(8,128)(2,1)}), bf16[32,8,16,128]{3,2,1,0:T(8,128)(2,1)S(1)}, u32[]{:S(2)}, u32[]{:S(2)}) async-start(bf16[32,8,16,128]{3,2,1,0:T(8,128)(2,1)} %bitcast.31), calls=%async_computation.2 | async-start | bytes 2097152 | tf_op jit(solution)/shard_map/all_to_all | solution.py:334
  101.6 8.6 %collective-permute-start.7 = (bf16[128,512]{1,0:T(8,128)(2,1)S(1)}, bf16[128,512]{1,0:T(8,128)(2,1)S(1)}, u32[]{:S(2)}, u32[]{:S(2)}) collective-permute-start(bf16[128,512]{1,0:T(8,128)(2,1)S(1)} %get-tuple-element.13), channel_id=1, source_target_pairs={{0,224},{32,0},{64,32},{96,64},{128,96},{160,128},{192,160},{224,1... | collective-permute-start | bytes 393224 | tf_op jit(solution)/shard_map/ppermute | solution.py:328
  102.8 11.7 %collective-permute-start.6 = (bf16[128,512]{1,0:T(8,128)(2,1)S(1)}, bf16[128,512]{1,0:T(8,128)(2,1)S(1)}, u32[]{:S(2)}, u32[]{:S(2)}) collective-permute-start(bf16[128,512]{1,0:T(8,128)(2,1)S(1)} %get-tuple-element.14), channel_id=1, source_target_pairs={{0,192},{32,224},{64,0},{96,32},{128,64},{160,96},{192,128},{224,1... | collective-permute-start | bytes 393224 | tf_op jit(solution)/shard_map/ppermute | solution.py:328
  102.8 13.5 %collective-permute-start.5 = (bf16[128,512]{1,0:T(8,128)(2,1)S(1)}, bf16[128,512]{1,0:T(8,128)(2,1)S(1)}, u32[]{:S(2)}, u32[]{:S(2)}) collective-permute-start(bf16[128,512]{1,0:T(8,128)(2,1)S(1)} %get-tuple-element.15), channel_id=1, source_target_pairs={{0,160},{32,192},{64,224},{96,0},{128,32},{160,64},{192,96},{224,1... | collective-permute-start | bytes 393224 | tf_op jit(solution)/shard_map/ppermute | solution.py:328
  105.7 10.7 %collective-permute-start.4 = (bf16[128,512]{1,0:T(8,128)(2,1)S(1)}, bf16[128,512]{1,0:T(8,128)(2,1)S(1)}, u32[]{:S(2)}, u32[]{:S(2)}) collective-permute-start(bf16[128,512]{1,0:T(8,128)(2,1)S(1)} %get-tuple-element.16), channel_id=1, source_target_pairs={{0,128},{32,160},{64,192},{96,224},{128,0},{160,32},{192,64},{224,... | collective-permute-start | bytes 393224 | tf_op jit(solution)/shard_map/ppermute | solution.py:328
  108.3 19.4 %collective-permute-start.3 = (bf16[128,512]{1,0:T(8,128)(2,1)S(1)}, bf16[128,512]{1,0:T(8,128)(2,1)S(1)}, u32[]{:S(2)}, u32[]{:S(2)}) collective-permute-start(bf16[128,512]{1,0:T(8,128)(2,1)S(1)} %get-tuple-element.17), channel_id=1, source_target_pairs={{0,96},{32,128},{64,160},{96,192},{128,224},{160,0},{192,32},{224,... | collective-permute-start | bytes 393224 | tf_op jit(solution)/shard_map/ppermute | solution.py:328
  110.3 17.4 %collective-permute-start.2 = (bf16[128,512]{1,0:T(8,128)(2,1)S(1)}, bf16[128,512]{1,0:T(8,128)(2,1)S(1)}, u32[]{:S(2)}, u32[]{:S(2)}) collective-permute-start(bf16[128,512]{1,0:T(8,128)(2,1)S(1)} %get-tuple-element.18), channel_id=1, source_target_pairs={{0,64},{32,96},{64,128},{96,160},{128,192},{160,224},{192,0},{224,... | collective-permute-start | bytes 393224 | tf_op jit(solution)/shard_map/ppermute | solution.py:328
  114.5 18.1 %collective-permute-start.1 = (bf16[128,512]{1,0:T(8,128)(2,1)S(1)}, bf16[128,512]{1,0:T(8,128)(2,1)S(1)}, u32[]{:S(2)}, u32[]{:S(2)}) collective-permute-start(bf16[128,512]{1,0:T(8,128)(2,1)S(1)} %get-tuple-element.19), channel_id=1, source_target_pairs={{0,32},{32,64},{64,96},{96,128},{128,160},{160,192},{192,224},{224... | collective-permute-start | bytes 393224 | tf_op jit(solution)/shard_map/ppermute | solution.py:328

commit v4 on v3

--- a/solution.py
+++ b/solution.py
@@ -9,8 +9,8 @@
 F32 = jnp.float32
 BF16 = jnp.bfloat16
 TILE = 128
-ROW_CHUNK = 512
-SPLIT = 4
+ROW_CHUNK = 1024
+SPLIT = 8
 MIB = 1024 * 1024
 SMALL = pltpu.CompilerParams(vmem_limit_bytes=16 * MIB)
 LARGE = pltpu.CompilerParams(vmem_limit_bytes=58 * MIB)
@@ -45,8 +45,13 @@
     earlier = taps - 1
     ones = identity(TILE)
 
-    def fetch(which):
-        return pltpu.make_async_copy(own_ref.at[which], x_ref.at[which], arrived.at[which])
+    share = own_ref.shape[2] // arrived.shape[1]
+
+    def fetch(which, index):
+        lanes = pl.ds(pl.multiple_of(index * share, share), share)
+        return pltpu.make_async_copy(
+            own_ref.at[which, :, lanes], x_ref.at[which, :, lanes], arrived.at[which, index]
+        )
 
     def leave(slot):
         turn = (slot + slots - here_ref[0]) % slots
@@ -58,12 +63,16 @@
             ),
         )
 
-    for which in range(streams):
-        fetch(which).start()
-    for which in range(streams):
-        fetch(which).wait()
+    for index in range(arrived.shape[1]):
+        for which in range(streams):
+            fetch(which, index).start()
 
     def step(slot, carry):
+        @pl.when(slot * columns % share == 0)
+        def _():
+            for which in range(streams):
+                fetch(which, slot * columns // share).wait()
+
         for part in range(parts):
             lanes = slice(part * TILE, (part + 1) * TILE)
             along = pl.ds(pl.multiple_of(slot * columns + part * TILE, TILE), TILE)
@@ -112,7 +121,7 @@
             pltpu.VMEM((streams * columns // TILE, rows + 8, TILE), F32),
             pltpu.VMEM((slots, rows, columns), BF16),
             pltpu.VMEM((slots, pieces, per_device, rows), BF16),
-            pltpu.SemaphoreType.DMA((streams,)),
+            pltpu.SemaphoreType.DMA((streams, 4)),
             pltpu.SemaphoreType.DMA((2, slots)),
         ],
         compiler_params=WIDE,
@@ -121,37 +130,47 @@
     )(here, own, before, taps)
 
 
-def toeplitz_kernel(lags_ref, out_ref, earlier_ref):
+def toeplitz_kernel(lags_ref, out_ref, made_ref, left):
+    batches = made_ref.shape[0]
     count, tile = lags_ref.shape
+    each = count // batches
     upper = lax.broadcasted_iota(jnp.int32, (tile, tile), 1) >= lax.broadcasted_iota(
         jnp.int32, (tile, tile), 0
     )
 
-    @pl.when(pl.program_id(0) == 0)
-    def _():
-        earlier_ref[...] = jnp.zeros_like(earlier_ref)
-
-    earlier = earlier_ref[...]
-    lines = lags_ref[...].astype(F32)
-    for part in range(count):
-        spread = jnp.broadcast_to(lines[part : part + 1], (tile, tile))
-        turned = pltpu.roll(spread, 0, 1, stride=1, stride_axis=0)
-        place = slice(part * tile, (part + 1) * tile)
-        out_ref[place, :] = jnp.where(upper, turned, earlier).astype(BF16)
-        earlier = turned
-    earlier_ref[...] = earlier
+    def leave(index):
+        size = each * tile
+        target = pl.ds(pl.multiple_of(index * size, size), size)
+        return pltpu.make_async_copy(made_ref.at[index], out_ref.at[target, :], left.at[index])
+
+    def step(index, earlier):
+        lines = lags_ref[pl.ds(pl.multiple_of(index * each, each), each), :].astype(F32)
+        for part in range(each):
+            spread = jnp.broadcast_to(lines[part : part + 1], (tile, tile))
+            turned = pltpu.roll(spread, 0, 1, stride=1, stride_axis=0)
+            place = slice(part * tile, (part + 1) * tile)
+            made_ref[index, place, :] = jnp.where(upper, turned, earlier).astype(BF16)
+            earlier = turned
+        leave(index).start()
+        return earlier
+
+    lax.fori_loop(0, batches, step, jnp.zeros((tile, tile), F32))
+    for index in range(batches):
+        leave(index).wait()
 
 
 def toeplitz(lags):
     count, tile = lags.shape
-    each = 16
+    batches = count // 16
     return pl.pallas_call(
         toeplitz_kernel,
-        grid=(count // each,),
         out_shape=jax.ShapeDtypeStruct((count * tile, tile), BF16),
-        in_specs=[pl.BlockSpec((each, tile), lambda i: (i, 0))],
-        out_specs=pl.BlockSpec((each * tile, tile), lambda i: (i, 0)),
-        scratch_shapes=[pltpu.VMEM((tile, tile), F32)],
+        in_specs=[WHOLE],
+        out_specs=FAR,
+        scratch_shapes=[
+            pltpu.VMEM((batches, count // batches * tile, tile), BF16),
+            pltpu.SemaphoreType.DMA((batches,)),
+        ],
         compiler_params=WIDE,
         cost_estimate=estimate(4 * count * tile * tile, 2 * count * tile * tile),
         name="toeplitz",

time: 135 us -> 133 us (0.985)
  Pallas kernels: 42.9 us -> 36.7 us
  waiting for transfers between devices: 46.7 us -> 51.7 us
    pallas_call x1, Pallas kernels: 10.3 us -> 5.4 us  [toeplitz(): pl.pallas_call(toeplitz_kernel, out_shape=jax.ShapeDtypeStruct((count * t...]
    all_to_all x1, waiting for transfers between devices: 20.1 us -> 25 us  [stages(): kv = lax.all_to_all(kv, ('chan', 'ctx'), 0, 0, tiled=True)]
  transfers between devices with their start and end apart: 11 -> 11, of which waited for: 6 -> 6; matrix products, arithmetic and copies ran while one was open for 1% -> 1% of each run, Pallas kernels for 13% -> 9%
where the time goes in v4:
time: 133 us
  waiting for transfers between devices  51.7 us (39%)
  starting transfers between devices  40.3 us (30%)
  Pallas kernels  36.7 us (28%)
  local copies, waits for them, and re-layouts  3.42 us (3%)
    all_to_all x1, waiting for transfers between devices, stages(): kv = lax.all_to_all(kv, ('chan', 'ctx'), 0, 0, tiled=True)  25 us
    pallas_call x1, Pallas kernels, convolve(): pl.pallas_call(convolve_kernel, out_shape=jax.ShapeDtypeStruct((blocks, c...  23.6 us
    ppermute x7, waiting for transfers between devices, stages(): queries.append(lax.ppermute(query[shift], 'chan', ring))  20.8 us
    all_to_all x1, starting transfers between devices, stages(): kv = lax.all_to_all(kv, ('chan', 'ctx'), 0, 0, tiled=True)  12.2 us
    ppermute x7, starting transfers between devices, stages(): queries.append(lax.ppermute(query[shift], 'chan', ring))  10.3 us
    all_to_all x1, starting transfers between devices, stages(): lines = lax.all_to_all(lines, 'ctx', 0, 0, tiled=True).reshape(-1, TILE)  8.58 us
    pallas_call x1, Pallas kernels, featurize(): pl.pallas_call(featurize_kernel, out_shape=(jax.ShapeDtypeStruct((slots,...  6.34 us
    ppermute x1, waiting for transfers between devices, stages(): before = lax.ppermute(own[:, rows - (lags - 1):], ('chan', 'ctx'), pairs)  5.92 us
  transfers between devices with their start and end apart: 11, of which 6 were waited for; matrix products, arithmetic and copies ran while one was open for 1% of the time, Pallas kernels for 9%

profile of v4, /device:TPU:1, one launch (start us, length us, event | category | flops | bytes accessed | tf_op | source)
XLA Modules:
  0.0 132.9 jit_solution(13662824743458668057)
XLA Ops:
  0.0 0.7 convert_bitcast_fusion
  0.7 0.6 copy.5
  1.4 8.6 %all-to-all-start = ((bf16[32,8,128]{2,1,0:T(8,128)(2,1)}), bf16[32,8,128]{2,1,0:T(8,128)(2,1)S(1)}, u32[]{:S(2)}, u32[]{:S(2)}) async-start(bf16[32,8,128]{2,1,0:T(8,128)(2,1)} %bitcast.19), calls=%async_computation | async-start | bytes 131072 | tf_op jit(solution)/shard_map/all_to_all | solution.py:338
  9.9 1.0 slice.36
  10.9 3.5 %collective-permute-start = (bf16[3,2,4096]{2,1,0:T(2,128)(2,1)S(1)}, bf16[3,2,4096]{2,1,0:T(2,128)(2,1)S(1)}, u32[]{:S(2)}, u32[]{:S(2)}) collective-permute-start(bf16[3,2,4096]{2,1,0:T(2,128)(2,1)S(1)} %slice.36), channel_id=1, source_target_pairs={{0,32},{32,64},{64,96},{96,128},{128,160},{160,192},{192,224},{224... | collective-permute-start | bytes 147464 | tf_op jit(solution)/shard_map/ppermute | solution.py:333
  14.5 5.9 %collective-permute-done.before_ref = bf16[3,2,4096]{2,1,0:T(2,128)(2,1)S(1)} collective-permute-done((bf16[3,2,4096]{2,1,0:T(2,128)(2,1)S(1)}, bf16[3,2,4096]{2,1,0:T(2,128)(2,1)S(1)}, u32[]{:S(2)}, u32[]{:S(2)}) %collective-permute-start) | collective-permute-done | bytes 49184 | tf_op jit(solution)/shard_map/ppermute | solution.py:333
  20.4 0.6 copy-done.3
  21.0 6.3 %featurize.1 = (bf16[8,128,512]{2,1,0:T(8,128)(2,1)}, bf16[256,16,128]{2,1,0:T(8,128)(2,1)}) custom-call(s32[1]{0:T(128)} %bitcast.here_ref, bf16[3,128,4096]{2,1,0:T(8,128)(2,1)} %bitcast.30, bf16[3,2,4096]{2,1,0:T(2,128)(2,1)} %copy-done.3, bf16[3,3,4096]{2,1,0:T(4,128)(2,1)} %taps_ref.1), custom_call_target="tpu_custom_call" | custom-call | flops 31457280 | bytes 6291456 | tf_op jit(solution)/shard_map/featurize/pallas_call | solution.py:111
  27.4 12.2 %all-to-all-start.1 = ((bf16[256,16,128]{2,1,0:T(8,128)(2,1)}), bf16[256,16,128]{2,1,0:T(8,128)(2,1)S(1)}, u32[]{:S(2)}, u32[]{:S(2)}) async-start(bf16[256,16,128]{2,1,0:T(8,128)(2,1)} %get-tuple-element.11), calls=%async_computation.1 | async-start | bytes 2097152 | tf_op jit(solution)/shard_map/all_to_all | solution.py:343
  39.6 5.4 %toeplitz.1.tiles_ref = bf16[32768,128]{1,0:T(8,128)(2,1)} custom-call(bf16[256,128]{1,0:T(8,128)(2,1)} %bitcast.33), custom_call_target="tpu_custom_call" | custom-call | flops 16777216 | bytes 8388608 | tf_op jit(solution)/shard_map/toeplitz/pallas_call | solution.py:165
  45.0 25.0 %all-to-all-done.1 = bf16[256,16,128]{2,1,0:T(8,128)(2,1)S(1)} async-done(((bf16[256,16,128]{2,1,0:T(8,128)(2,1)}), bf16[256,16,128]{2,1,0:T(8,128)(2,1)S(1)}, u32[]{:S(2)}, u32[]{:S(2)}) %all-to-all-start.1) | async-done | bytes 1048608 | tf_op jit(solution)/shard_map/all_to_all | solution.py:343
  70.0 1.1 copy-done.1
  71.0 23.6 %convolve.1 = bf16[256,16,128]{2,1,0:T(8,128)(2,1)} custom-call(s32[1]{0:T(128)} %bitcast.12.here_ref, f32[512]{0:T(512)} %gain_ref.1, bf16[8,32,16,128]{3,2,1,0:T(8,128)(2,1)} %bitcast.32, bf16[32768,128]{1,0:T(8,128)(2,1)} %toeplitz.1.tiles_ref), custom_call_target="tpu_custom_call" | custom-call | flops 17179869184 | bytes 10485760 | tf_op jit(solution)/shard_map/convolve/pallas_call | solution.py:276
  94.6 5.6 %all-to-all-start.2 = ((bf16[32,8,16,128]{3,2,1,0:T(8,128)(2,1)}), bf16[32,8,16,128]{3,2,1,0:T(8,128)(2,1)S(1)}, u32[]{:S(2)}, u32[]{:S(2)}) async-start(bf16[32,8,16,128]{3,2,1,0:T(8,128)(2,1)} %bitcast.31), calls=%async_computation.2 | async-start | bytes 2097152 | tf_op jit(solution)/shard_map/all_to_all | solution.py:353
  100.4 1.2 collective-permute-start.7
  101.6 2.9 %collective-permute-start.5 = (bf16[128,512]{1,0:T(8,128)(2,1)S(1)}, bf16[128,512]{1,0:T(8,128)(2,1)S(1)}, u32[]{:S(2)}, u32[]{:S(2)}) collective-permute-start(bf16[128,512]{1,0:T(8,128)(2,1)S(1)} %get-tuple-element.15), channel_id=1, source_target_pairs={{0,160},{32,192},{64,224},{96,0},{128,32},{160,64},{192,96},{224,1... | collective-permute-start | bytes 393224 | tf_op jit(solution)/shard_map/ppermute | solution.py:347
  104.4 2.8 %collective-permute-start.4 = (bf16[128,512]{1,0:T(8,128)(2,1)S(1)}, bf16[128,512]{1,0:T(8,128)(2,1)S(1)}, u32[]{:S(2)}, u32[]{:S(2)}) collective-permute-start(bf16[128,512]{1,0:T(8,128)(2,1)S(1)} %get-tuple-element.16), channel_id=1, source_target_pairs={{0,128},{32,160},{64,192},{96,224},{128,0},{160,32},{192,64},{224,... | collective-permute-start | bytes 393224 | tf_op jit(solution)/shard_map/ppermute | solution.py:347
  107.2 1.8 %collective-permute-start.3 = (bf16[128,512]{1,0:T(8,128)(2,1)S(1)}, bf16[128,512]{1,0:T(8,128)(2,1)S(1)}, u32[]{:S(2)}, u32[]{:S(2)}) collective-permute-start(bf16[128,512]{1,0:T(8,128)(2,1)S(1)} %get-tuple-element.17), channel_id=1, source_target_pairs={{0,96},{32,128},{64,160},{96,192},{128,224},{160,0},{192,32},{224,... | collective-permute-start | bytes 393224 | tf_op jit(solution)/shard_map/ppermute | solution.py:347
  109.0 1.7 %collective-permute-start.2 = (bf16[128,512]{1,0:T(8,128)(2,1)S(1)}, bf16[128,512]{1,0:T(8,128)(2,1)S(1)}, u32[]{:S(2)}, u32[]{:S(2)}) collective-permute-start(bf16[128,512]{1,0:T(8,128)(2,1)S(1)} %get-tuple-element.18), channel_id=1, source_target_pairs={{0,64},{32,96},{64,128},{96,160},{128,192},{160,224},{192,0},{224,... | collective-permute-start | bytes 393224 | tf_op jit(solution)/shard_map/ppermute | solution.py:347
  110.7 2.5 %collective-permute-done.6.refs_6_ = bf16[128,512]{1,0:T(8,128)(2,1)S(1)} collective-permute-done((bf16[128,512]{1,0:T(8,128)(2,1)S(1)}, bf16[128,512]{1,0:T(8,128)(2,1)S(1)}, u32[]{:S(2)}, u32[]{:S(2)}) %collective-permute-start.6) | collective-permute-done | bytes 131104 | tf_op jit(solution)/shard_map/ppermute | solution.py:347
  113.3 1.8 %collective-permute-done.5.refs_5_ = bf16[128,512]{1,0:T(8,128)(2,1)S(1)} collective-permute-done((bf16[128,512]{1,0:T(8,128)(2,1)S(1)}, bf16[128,512]{1,0:T(8,128)(2,1)S(1)}, u32[]{:S(2)}, u32[]{:S(2)}) %collective-permute-start.5) | collective-permute-done | bytes 131104 | tf_op jit(solution)/shard_map/ppermute | solution.py:347
  115.1 11.3 %collective-permute-done.3.refs_3_ = bf16[128,512]{1,0:T(8,128)(2,1)S(1)} collective-permute-done((bf16[128,512]{1,0:T(8,128)(2,1)S(1)}, bf16[128,512]{1,0:T(8,128)(2,1)S(1)}, u32[]{:S(2)}, u32[]{:S(2)}) %collective-permute-start.3) | collective-permute-done | bytes 131104 | tf_op jit(solution)/shard_map/ppermute | solution.py:347
  126.4 5.1 %collective-permute-done.1.refs_1_ = bf16[128,512]{1,0:T(8,128)(2,1)S(1)} collective-permute-done((bf16[128,512]{1,0:T(8,128)(2,1)S(1)}, bf16[128,512]{1,0:T(8,128)(2,1)S(1)}, u32[]{:S(2)}, u32[]{:S(2)}) %collective-permute-start.1) | collective-permute-done | bytes 131104 | tf_op jit(solution)/shard_map/ppermute | solution.py:347
  131.5 1.4 %gate.1 = bf16[1024,512]{1,0:T(8,128)(2,1)} custom-call(s32[1]{0:T(128)} %bitcast.here_ref, bf16[128,512]{1,0:T(8,128)(2,1)S(1)} %get-tuple-element.20.refs_0_, bf16[128,512]{1,0:T(8,128)(2,1)S(1)} %collective-permute-done.1.refs_1_, bf16[128,512]{1,0:T(8,128)(2,1)S(1)} %collective-permute-done.2.refs_2_, ...), custom_call_target="tpu_custom_call" | custom-call | flops 1048576 | bytes 3145728 | tf_op jit(solution)/shard_map/gate/pallas_call | solution.py:310
  (15 shorter events, 0.1 us)
Async XLA Ops:
  1.4 26.0 %all-to-all-start = ((bf16[32,8,128]{2,1,0:T(8,128)(2,1)}), bf16[32,8,128]{2,1,0:T(8,128)(2,1)S(1)}, u32[]{:S(2)}, u32[]{:S(2)}) async-start(bf16[32,8,128]{2,1,0:T(8,128)(2,1)} %bitcast.19), calls=%async_computation | async-start | bytes 131072 | tf_op jit(solution)/shard_map/all_to_all | solution.py:338
  10.9 9.5 %collective-permute-start = (bf16[3,2,4096]{2,1,0:T(2,128)(2,1)S(1)}, bf16[3,2,4096]{2,1,0:T(2,128)(2,1)S(1)}, u32[]{:S(2)}, u32[]{:S(2)}) collective-permute-start(bf16[3,2,4096]{2,1,0:T(2,128)(2,1)S(1)} %slice.36), channel_id=1, source_target_pairs={{0,32},{32,64},{64,96},{96,128},{128,160},{160,192},{192,224},{224... | collective-permute-start | bytes 147464 | tf_op jit(solution)/shard_map/ppermute | solution.py:333
  20.4 0.6 copy-start.3
  27.4 12.2 %copy-start.2 = (bf16[32,8,128]{2,1,0:T(8,128)(2,1)}, bf16[32,8,128]{2,1,0:T(8,128)(2,1)S(1)}, u32[]{:S(2)}) copy-start(bf16[32,8,128]{2,1,0:T(8,128)(2,1)S(1)} %all-to-all-done) | copy-start | bytes 196612
  27.4 42.6 %all-to-all-start.1 = ((bf16[256,16,128]{2,1,0:T(8,128)(2,1)}), bf16[256,16,128]{2,1,0:T(8,128)(2,1)S(1)}, u32[]{:S(2)}, u32[]{:S(2)}) async-start(bf16[256,16,128]{2,1,0:T(8,128)(2,1)} %get-tuple-element.11), calls=%async_computation.1 | async-start | bytes 2097152 | tf_op jit(solution)/shard_map/all_to_all | solution.py:343
  70.0 1.1 copy-start.1
  71.0 29.2 %copy-start = (bf16[8,128,512]{2,1,0:T(8,128)(2,1)S(1)}, bf16[8,128,512]{2,1,0:T(8,128)(2,1)}, u32[]{:S(2)}) copy-start(bf16[8,128,512]{2,1,0:T(8,128)(2,1)} %get-tuple-element.9) | copy-start | bytes 3145732
  94.6 36.9 %all-to-all-start.2 = ((bf16[32,8,16,128]{3,2,1,0:T(8,128)(2,1)}), bf16[32,8,16,128]{3,2,1,0:T(8,128)(2,1)S(1)}, u32[]{:S(2)}, u32[]{:S(2)}) async-start(bf16[32,8,16,128]{3,2,1,0:T(8,128)(2,1)} %bitcast.31), calls=%async_computation.2 | async-start | bytes 2097152 | tf_op jit(solution)/shard_map/all_to_all | solution.py:353
  100.4 8.6 %collective-permute-start.7 = (bf16[128,512]{1,0:T(8,128)(2,1)S(1)}, bf16[128,512]{1,0:T(8,128)(2,1)S(1)}, u32[]{:S(2)}, u32[]{:S(2)}) collective-permute-start(bf16[128,512]{1,0:T(8,128)(2,1)S(1)} %get-tuple-element.13), channel_id=1, source_target_pairs={{0,224},{32,0},{64,32},{96,64},{128,96},{160,128},{192,160},{224,1... | collective-permute-start | bytes 393224 | tf_op jit(solution)/shard_map/ppermute | solution.py:347
  101.6 11.7 %collective-permute-start.6 = (bf16[128,512]{1,0:T(8,128)(2,1)S(1)}, bf16[128,512]{1,0:T(8,128)(2,1)S(1)}, u32[]{:S(2)}, u32[]{:S(2)}) collective-permute-start(bf16[128,512]{1,0:T(8,128)(2,1)S(1)} %get-tuple-element.14), channel_id=1, source_target_pairs={{0,192},{32,224},{64,0},{96,32},{128,64},{160,96},{192,128},{224,1... | collective-permute-start | bytes 393224 | tf_op jit(solution)/shard_map/ppermute | solution.py:347
  101.6 13.5 %collective-permute-start.5 = (bf16[128,512]{1,0:T(8,128)(2,1)S(1)}, bf16[128,512]{1,0:T(8,128)(2,1)S(1)}, u32[]{:S(2)}, u32[]{:S(2)}) collective-permute-start(bf16[128,512]{1,0:T(8,128)(2,1)S(1)} %get-tuple-element.15), channel_id=1, source_target_pairs={{0,160},{32,192},{64,224},{96,0},{128,32},{160,64},{192,96},{224,1... | collective-permute-start | bytes 393224 | tf_op jit(solution)/shard_map/ppermute | solution.py:347
  104.4 10.7 %collective-permute-start.4 = (bf16[128,512]{1,0:T(8,128)(2,1)S(1)}, bf16[128,512]{1,0:T(8,128)(2,1)S(1)}, u32[]{:S(2)}, u32[]{:S(2)}) collective-permute-start(bf16[128,512]{1,0:T(8,128)(2,1)S(1)} %get-tuple-element.16), channel_id=1, source_target_pairs={{0,128},{32,160},{64,192},{96,224},{128,0},{160,32},{192,64},{224,... | collective-permute-start | bytes 393224 | tf_op jit(solution)/shard_map/ppermute | solution.py:347
  107.2 19.2 %collective-permute-start.3 = (bf16[128,512]{1,0:T(8,128)(2,1)S(1)}, bf16[128,512]{1,0:T(8,128)(2,1)S(1)}, u32[]{:S(2)}, u32[]{:S(2)}) collective-permute-start(bf16[128,512]{1,0:T(8,128)(2,1)S(1)} %get-tuple-element.17), channel_id=1, source_target_pairs={{0,96},{32,128},{64,160},{96,192},{128,224},{160,0},{192,32},{224,... | collective-permute-start | bytes 393224 | tf_op jit(solution)/shard_map/ppermute | solution.py:347
  109.0 17.4 %collective-permute-start.2 = (bf16[128,512]{1,0:T(8,128)(2,1)S(1)}, bf16[128,512]{1,0:T(8,128)(2,1)S(1)}, u32[]{:S(2)}, u32[]{:S(2)}) collective-permute-start(bf16[128,512]{1,0:T(8,128)(2,1)S(1)} %get-tuple-element.18), channel_id=1, source_target_pairs={{0,64},{32,96},{64,128},{96,160},{128,192},{160,224},{192,0},{224,... | collective-permute-start | bytes 393224 | tf_op jit(solution)/shard_map/ppermute | solution.py:347
  113.3 18.2 %collective-permute-start.1 = (bf16[128,512]{1,0:T(8,128)(2,1)S(1)}, bf16[128,512]{1,0:T(8,128)(2,1)S(1)}, u32[]{:S(2)}, u32[]{:S(2)}) collective-permute-start(bf16[128,512]{1,0:T(8,128)(2,1)S(1)} %get-tuple-element.19), channel_id=1, source_target_pairs={{0,32},{32,64},{64,96},{96,128},{128,160},{160,192},{192,224},{224... | collective-permute-start | bytes 393224 | tf_op jit(solution)/shard_map/ppermute | solution.py:347
